TPU v7x, 256 devices: a whole 4x4x8 slice. The times are simulated.
256 devices in a mesh: dom: 64 (over x, z, y_lo), feat: 4 (over y_hi, core).
Axes of the slice: x: 4, y: 4 (y_hi: 2, y_lo: 2; y = y_hi * 2 + y_lo), z: 8, core: 2. Of those that a mesh axis runs over, the one named last changes fastest.
Arguments:
- embed: bfloat16 [256, 65536], P('feat', 'dom'), may hold values from -6 to 6
- weight: bfloat16 [256, 256], P('feat'), may hold values from -0.375 to 0.375
- cotangent: bfloat16 [256, 65536], P('feat', 'dom'), may hold values from -6 to 6
- edge_masks: int32 [6144, 128, 128], P('dom'), may hold values 0 or 1
- tile_rows: int32 [6144], P('dom'), may hold values from 0 to 7
- tile_owner: int32 [6144, 1], P('dom'), may hold values from 0 to 63; in each aligned block of 96 rows (0 to 95, 96 to 191, ...) at most 2 rows name the same one
- tile_sub: int32 [6144], P('dom'), may hold values from 0 to 7
Outputs:
- output: bfloat16 [256, 65536], P('feat', 'dom')
- embed_grad: float32 [256, 65536], P('feat', 'dom')
- weight_grad: float32 [256, 256], P('feat')
Inputs may be any that keep to these rules, and one draw needn't show every extreme that they name: `tile_owner`: among the 96 tiles of one index of dom no owner is named more than 2 times, a bound that some block reaches.
All inputs are finite; a program needn't handle non-finite values. No bound on the sum of `edge_masks` on one device may be relied on, other than what follows from the above.
Results may differ from a plain program's by a relative error of at most 0.0059.
Values may be sent and summed in bfloat16 or wider, within the bound.
No kernel may reach another device: no remote copies, remote signals or barrier semaphores. Data moves between devices by JAX's collectives and lax.ppermute only.
A program may use at most 64 MiB of HBM per device.

v0:
```python
import math

import jax
import jax.numpy as jnp
from jax import lax
from jax.sharding import PartitionSpec as P


def per_device(embed, weight, cotangent, edge_masks, tile_rows, tile_owner, tile_sub):
    feat_width = embed.shape[0]
    local_nodes = embed.shape[1]
    block_len = edge_masks.shape[1]
    local_blocks = local_nodes // block_len
    dom_count = lax.axis_size("dom")
    nodes_all = local_nodes * dom_count
    block_range = jnp.arange(local_blocks, dtype=jnp.int32)
    col_ids = tile_owner[:, 0] * local_blocks + tile_sub
    own_bf = embed.reshape(feat_width, local_blocks, block_len)
    gathered = lax.all_gather(embed, "dom", axis=1, tiled=True)
    all_blocks = gathered.reshape(feat_width, dom_count * local_blocks, block_len)
    fetched = jnp.take(all_blocks, col_ids, axis=1)
    mask_bf = edge_masks.astype(jnp.bfloat16)
    contrib = jnp.einsum("ftj,tij->fti", fetched, mask_bf, preferred_element_type=jnp.float32)
    row_onehot = (tile_rows[:, None] == block_range[None, :]).astype(jnp.float32)
    neighbour = jnp.einsum("fti,tr->fri", contrib, row_onehot, precision=lax.Precision.HIGHEST)
    row_int = (tile_rows[:, None] == block_range[None, :]).astype(jnp.int32)
    counts = jnp.sum(edge_masks, axis=2)
    degree = jnp.dot(row_int.T, counts)
    inv_root = 1.0 / jnp.sqrt(1.0 + degree.astype(jnp.float32))
    own_blocks = own_bf.astype(jnp.float32)
    aggregate = (
        (own_blocks + neighbour * inv_root[None])
        .astype(jnp.bfloat16)
        .reshape(feat_width, local_nodes)
    )
    pre_act = lax.psum_scatter(
        jnp.einsum("fh,fn->hn", weight, aggregate, preferred_element_type=jnp.float32),
        "feat",
        scatter_dimension=0,
        tiled=True,
    )
    gate_vals = jax.nn.sigmoid(pre_act)
    output = (pre_act * gate_vals).astype(jnp.bfloat16)
    grad_pre = (
        cotangent.astype(jnp.float32) * gate_vals * (1.0 + pre_act * (1.0 - gate_vals))
    ).astype(jnp.bfloat16)
    grad_full = lax.all_gather(grad_pre, "feat", axis=0, tiled=True)
    grad_agg = jnp.einsum("fh,hn->fn", weight, grad_full, preferred_element_type=jnp.float32)
    weight_terms = jnp.einsum("fn,hn->fh", aggregate, grad_full, preferred_element_type=jnp.float32)
    grad_blocks = grad_agg.reshape(feat_width, local_blocks, block_len)
    scaled_grad = (grad_blocks * inv_root[None]).astype(jnp.bfloat16)
    selected = jnp.take(scaled_grad, tile_rows, axis=1)
    partials = jnp.einsum("fti,tij->tfj", selected, mask_bf, preferred_element_type=jnp.float32)
    start = jnp.int32(0)
    inside = (col_ids >= start) & (col_ids < start + lax.axis_size("dom") * local_blocks)
    target = jnp.where(inside, col_ids, lax.axis_size("dom") * local_blocks)
    empty = jnp.zeros((lax.axis_size("dom") * local_blocks, feat_width, block_len), jnp.float32)
    received = lax.psum_scatter(
        empty.at[target].add(partials, mode="drop"), "dom", scatter_dimension=0, tiled=True
    )
    incoming = jnp.transpose(received, (1, 0, 2))
    embed_grad = (grad_blocks + incoming).reshape(feat_width, local_nodes)
    weight_grad = lax.psum(weight_terms, "dom") / math.sqrt(nodes_all)
    return (output, embed_grad, weight_grad)


def solution(mesh):
    in_specs = (
        P("feat", "dom"),
        P("feat", None),
        P("feat", "dom"),
        P("dom", None, None),
        P("dom"),
        P("dom", None),
        P("dom"),
    )
    out_specs = (P("feat", "dom"), P("feat", "dom"), P("feat", None))
    return jax.shard_map(
        per_device, mesh=mesh, in_specs=in_specs, out_specs=out_specs, check_vma=False
    )
```

profile of v0, /device:TPU:8, one launch (start us, length us, event | category | flops | bytes accessed | tf_op | source)
XLA Modules:
  0.0 1293.9 jit_solution(5123875509077076049)
XLA Ops:
  7.2 0.0 copy-start
  7.2 0.0 all-gather.2.cloned.1.call-start
  7.2 0.7 all-gather.2.cloned.1.call-update
  7.9 0.0 reduce-scatter.7.cloned.1.call-start
  8.0 0.9 convert_bitcast_fusion
  9.0 4.5 reduce_sum.9
  13.5 0.1 fusion.24
  13.7 310.7 %all-gather.2.cloned.1.call-done = bf16[64,65536]{1,0:T(8,128)(2,1)} async-done(((bf16[64,1024]{1,0:T(8,128)(2,1)}), bf16[64,65536]{1,0:T(8,128)(2,1)}) %all-gather.2.cloned.1.call-update) | async-done | bytes 8388624 | tf_op jit(solution)/shard_map/all_gather | solution.py:19
  324.4 9.0 copy_bitcast_fusion
  333.4 4.2 gather_fusion
  337.7 5.0 convolution_bitcast_fusion
  342.7 2.9 fusion.20
  345.6 0.3 convolution_bitcast_fusion.1
  345.9 1.3 copy.39
  347.2 0.0 reduce-scatter.7.cloned.1.call-update
  347.2 0.0 all-reduce.2.cloned.1.call-start
  347.4 35.3 %reduce-scatter.7.cloned.1.call-done = f32[64,1024]{1,0:T(8,128)} async-done(((f32[256,1024]{1,0:T(8,128)}), f32[64,1024]{1,0:T(8,128)}) %reduce-scatter.7.cloned.1.call-update) | async-done | bytes 262160 | tf_op jit(solution)/shard_map/reduce_scatter | solution.py:36
  382.7 1.7 multiply_convert_fusion
  384.4 8.3 all_gather.7
  392.6 0.9 fusion.29
  393.6 0.2 convolution_bitcast_fusion.2
  393.8 0.0 all-reduce.2.cloned.1.call-update
  393.8 0.2 reduce-scatter.5.cloned.1.call-start
  394.0 2.0 gather_fusion.1
  396.0 4.3 fusion.2
  400.3 7.9 broadcast_in_dim.39
  408.2 13.5 %scatter_fusion = f32[512,64,128]{2,1,0:T(8,128)} fusion(f32[512,64,128]{2,1,0:T(8,128)} %broadcast_in_dim.39, s32[96]{0:T(128)S(1)} %compare_select_fusion.1, f32[96,64,128]{2,1,0:T(8,128)S(1)} %fusion.2), kind=kCustom, calls=%fused_computation.2 | custom fusion | flops 786432 | bytes 9437568 | tf_op jit(solution)/shard_map/scatter-add | solution.py:59
  421.7 0.0 reduce-scatter.5.cloned.1.call-update
  421.7 496.4 %all-reduce.2.cloned.1.call-done = f32[64,256]{1,0:T(8,128)} async-done(((f32[64,256]{1,0:T(8,128)}), f32[64,256]{1,0:T(8,128)}) %all-reduce.2.cloned.1.call-update) | async-done | bytes 65552 | tf_op jit(solution)/shard_map/psum | solution.py:63
  918.1 1.5 broadcast_multiply_fusion
  919.6 366.1 %reduce-scatter.5.cloned.1.call-done = f32[8,64,128]{2,1,0:T(8,128)} async-done(((f32[512,64,128]{2,1,0:T(8,128)}), f32[8,64,128]{2,1,0:T(8,128)}) %reduce-scatter.5.cloned.1.call-update) | async-done | bytes 262160 | tf_op jit(solution)/shard_map/reduce_scatter | solution.py:58
  1285.7 1.7 copy_bitcast_fusion.1
  (17 shorter events, 0.1 us)
Async XLA Ops:
  7.2 338.4 %copy-start = (bf16[64,256]{1,0:T(8,128)(2,1)S(1)}, bf16[64,256]{1,0:T(8,128)(2,1)}, u32[]{:S(2)}) copy-start(bf16[64,256]{1,0:T(8,128)(2,1)} %param.8) | copy-start | bytes 98308
  7.2 317.2 %all-gather.2.cloned.1.call-start = ((), (), s32[]{:S(2)}) async-start(), calls=%async_computation.2 | async-start | bytes 8519680 | tf_op jit(solution)/shard_map/all_gather | solution.py:19
  7.9 374.7 %reduce-scatter.7.cloned.1.call-start = ((), (), s32[]{:S(2)}) async-start(), calls=%async_computation.5 | async-start | bytes 1310720 | tf_op jit(solution)/shard_map/reduce_scatter | solution.py:36
  8.9 4.5 copy-start.3
  9.0 4.5 copy-start.4
  9.0 4.6 copy-start.2
  342.7 40.0 %copy-start.1 = (bf16[64,1024]{1,0:T(8,128)(2,1)S(1)}, bf16[64,1024]{1,0:T(8,128)(2,1)}, u32[]{:S(2)}) copy-start(bf16[64,1024]{1,0:T(8,128)(2,1)} %param.9) | copy-start | bytes 393220
  347.2 570.8 %all-reduce.2.cloned.1.call-start = ((), (), s32[]{:S(2)}) async-start(), calls=%async_computation.4 | async-start | bytes 131072 | tf_op jit(solution)/shard_map/psum | solution.py:63
  393.8 891.9 %reduce-scatter.5.cloned.1.call-start = ((), (), s32[]{:S(2)}) async-start(), calls=%async_computation.3 | async-start | bytes 17039360 | tf_op jit(solution)/shard_map/reduce_scatter | solution.py:58
Sparse Core Ops, SparseCore 0:
  9.8 314.5 all-gather.1
  347.4 35.2 reduce-scatter.6
  393.9 524.1 all-reduce.1
  920.5 365.1 reduce-scatter.4
where the time goes:
time: 1300 us; the launch traced here: 1290 us
  waiting for transfers between devices  1210 us (93%)
  local copies, waits for them, and re-layouts  24.5 us (2%)
  other arithmetic  23.9 us (2%)
  between operations  13.9 us (1%)
  matrix products  13.8 us (1%)
    psum x1, waiting for transfers between devices, per_device(): weight_grad = lax.psum(weight_terms, 'dom') / math.sqrt(nodes_all)  496 us
    reduce_scatter x1, waiting for transfers between devices, per_device(): lax.psum_scatter(empty.at[target].add(partials, mode='drop'), 'dom', scat...  366 us
    all_gather x1, waiting for transfers between devices, per_device(): gathered = lax.all_gather(embed, 'dom', axis=1, tiled=True)  311 us
    reduce_scatter x1, waiting for transfers between devices, per_device(): lax.psum_scatter(jnp.einsum('fh,fn->hn', weight, aggregate, preferred_ele...  35.3 us
  transfers between devices with their start and end apart: 4, of which 4 were waited for; matrix products, arithmetic and copies ran while one was open for 3% of the time, Pallas kernels for 0%

commit v1 on v0

v1 whole, which is shorter than its diff:
```python
import functools
import math

import jax
import jax.numpy as jnp
from jax import lax
from jax.experimental import pallas as pl
from jax.experimental.pallas import tpu as pltpu
from jax.sharding import PartitionSpec as P

F32 = jnp.float32
BF16 = jnp.bfloat16
VM = pl.BlockSpec(memory_space=pltpu.VMEM)
SM = pl.BlockSpec(memory_space=pltpu.SMEM)


def params(mib):
    return pltpu.CompilerParams(vmem_limit_bytes=mib << 20)


def cost(flops, moved, exps=0):
    return pl.CostEstimate(flops=flops, bytes_accessed=moved, transcendentals=exps)


def slots_kernel(owner_ref, sub_ref, ask_ref, slot_ref):
    owners = ask_ref.shape[0]
    tiles = owner_ref.shape[1]
    ids = lax.broadcasted_iota(jnp.int32, (owners, tiles), 0)
    hit = ids == owner_ref[...]
    earlier = lax.broadcasted_iota(jnp.int32, (tiles, tiles), 0) < lax.broadcasted_iota(
        jnp.int32, (tiles, tiles), 1
    )
    before = jnp.dot(
        hit.astype(F32).astype(BF16), earlier.astype(F32).astype(BF16), preferred_element_type=F32
    )
    sub = sub_ref[...].astype(F32)
    first = jnp.sum(jnp.where(hit & (before < 0.5), sub, 0.0), axis=1, keepdims=True)
    second = jnp.sum(jnp.where(hit & (before > 0.5), sub, 0.0), axis=1, keepdims=True)
    lane = lax.broadcasted_iota(jnp.int32, ask_ref.shape, 1)
    ask_ref[...] = jnp.where(lane == 0, first, jnp.where(lane == 1, second, 0.0)).astype(jnp.int32)
    slot_ref[...] = jnp.sum(
        jnp.where(hit, 2.0 * ids.astype(F32) + before, 0.0), axis=0, keepdims=True
    ).astype(jnp.int32)


def select_kernel(want_ref, own_ref, send_ref):
    readers = want_ref.shape[0]
    width = send_ref.shape[2]

    def body(step, carry):
        for j in range(8):
            reader = step * 8 + j
            for k in range(2):
                start = pl.multiple_of(want_ref[reader, k] * width, width)
                send_ref[reader * 2 + k] = own_ref[:, pl.ds(start, width)]
        return carry

    lax.fori_loop(0, readers // 8, body, 0)


def masks_kernel(rows_ref, edge_ref, mask_ref, root_ref, degree_ref):
    step = pl.program_id(0)
    many = edge_ref.shape[0]

    @pl.when(step == 0)
    def _():
        degree_ref[...] = jnp.zeros_like(degree_ref)

    ones = jnp.ones((8, edge_ref.shape[2]), BF16)
    for j in range(many):
        mask = edge_ref[j].astype(F32).astype(BF16)
        mask_ref[j] = mask
        count = lax.dot_general(ones, mask, (((1,), (1,)), ((), ())), preferred_element_type=F32)
        row = rows_ref[step * many + j]
        degree_ref[row] = degree_ref[row] + count

    @pl.when(step == pl.num_programs(0) - 1)
    def _():
        root_ref[...] = 1.0 / jnp.sqrt(1.0 + degree_ref[...])


def forward_kernel(slot_ref, rows_ref, got_ref, mask_ref, own_ref, root_ref, agg_ref, acc_ref):
    tiles = mask_ref.shape[0]
    blocks, _, width = acc_ref.shape
    acc_ref[...] = jnp.zeros_like(acc_ref)
    group = 8

    def body(step, carry):
        terms = []
        for j in range(group):
            tile = step * group + j
            terms.append(
                lax.dot_general(
                    got_ref[slot_ref[tile]],
                    mask_ref[tile],
                    (((1,), (1,)), ((), ())),
                    preferred_element_type=F32,
                )
            )
        for j in range(group):
            row = rows_ref[step * group + j]
            acc_ref[row] = acc_ref[row] + terms[j]
        return carry

    lax.fori_loop(0, tiles // group, body, 0)
    for r in range(blocks):
        cols = slice(r * width, (r + 1) * width)
        agg_ref[:, cols] = (
            own_ref[:, cols].astype(F32) + acc_ref[r] * root_ref[r, 0:1, :]
        ).astype(BF16)


def dense_kernel(
    part_ref, agg_ref, aggown_ref, full_ref, weight_ref, root_ref,
    out_ref, grad_ref, scaled_ref, terms_ref, act_ref,
):
    nodes = agg_ref.shape[1]
    feats = weight_ref.shape[0]
    width = scaled_ref.shape[2]
    first = pl.multiple_of(part_ref[0] * feats, feats)
    chunk = 2 * width
    terms = jnp.zeros(terms_ref.shape, F32)
    for c in range(nodes // chunk):
        cols = slice(c * chunk, (c + 1) * chunk)
        pre = lax.dot_general(
            full_ref[:, nodes:], agg_ref[:, cols], (((0,), (0,)), ((), ())), preferred_element_type=F32
        )
        gate = jax.nn.sigmoid(pre)
        act_ref[...] = pre * gate
        out_ref[:, cols] = act_ref[pl.ds(first, feats), :].astype(BF16)
        grad_pre = (full_ref[:, cols].astype(F32) * gate * (1.0 + pre * (1.0 - gate))).astype(BF16)
        grad = jnp.dot(weight_ref[...], grad_pre, preferred_element_type=F32)
        grad_ref[:, cols] = grad
        terms = terms + lax.dot_general(
            aggown_ref[:, cols], grad_pre, (((1,), (1,)), ((), ())), preferred_element_type=F32
        )
        for k in range(2):
            r = 2 * c + k
            scaled_ref[r] = (grad[:, k * width:(k + 1) * width] * root_ref[r, 0:1, :]).astype(BF16)
    terms_ref[...] = terms


def backward_kernel(slot_ref, rows_ref, scaled_ref, mask_ref, send_ref):
    tiles = mask_ref.shape[0]
    group = 8
    send_ref[...] = jnp.zeros_like(send_ref)

    def body(step, carry):
        for j in range(group):
            tile = step * group + j
            send_ref[slot_ref[tile]] = jnp.dot(
                scaled_ref[rows_ref[tile]], mask_ref[tile], preferred_element_type=F32
            ).astype(BF16)
        return carry

    lax.fori_loop(0, tiles // group, body, 0)


def combine_kernel(want_ref, got_ref, grad_ref, out_ref, acc_ref):
    blocks, _, width = acc_ref.shape
    readers = want_ref.shape[0]
    for r in range(blocks):
        acc_ref[r] = grad_ref[:, r * width:(r + 1) * width]

    def body(step, carry):
        for j in range(8):
            reader = step * 8 + j
            for k in range(2):
                block = want_ref[reader, k]
                acc_ref[block] = acc_ref[block] + got_ref[reader * 2 + k].astype(F32)
        return carry

    lax.fori_loop(0, readers // 8, body, 0)
    for r in range(blocks):
        out_ref[:, r * width:(r + 1) * width] = acc_ref[r]


def per_device(embed, weight, cotangent, edge_masks, tile_rows, tile_owner, tile_sub):
    feats, nodes = embed.shape
    tiles, width, _ = edge_masks.shape
    blocks = nodes // width
    n_dom = lax.axis_size("dom")
    n_feat = lax.axis_size("feat")
    hidden = weight.shape[1]
    shape = jax.ShapeDtypeStruct
    swap = functools.partial(lax.all_to_all, axis_name="dom", split_axis=0, concat_axis=0, tiled=True)

    ask, slot = pl.pallas_call(
        slots_kernel,
        out_shape=(shape((n_dom, 128), jnp.int32), shape((1, tiles), jnp.int32)),
        in_specs=[VM, VM],
        out_specs=(VM, VM),
        compiler_params=params(4),
        name="slots",
    )(tile_owner.reshape(1, tiles), tile_sub.reshape(1, tiles))
    slot = slot.reshape(tiles)
    want = swap(ask)

    send = pl.pallas_call(
        select_kernel,
        out_shape=shape((2 * n_dom, feats, width), BF16),
        in_specs=[SM, VM],
        out_specs=VM,
        compiler_params=params(8),
        cost_estimate=cost(0, 2 * 2 * n_dom * feats * width * 2),
        name="select",
    )(want, embed)
    got = swap(send)

    full = lax.all_gather(jnp.concatenate([cotangent, weight], axis=1), "feat", axis=0, tiled=True)
    many = math.gcd(tiles, 12)
    mask, root = pl.pallas_call(
        masks_kernel,
        out_shape=(shape(edge_masks.shape, BF16), shape((blocks, 8, width), F32)),
        grid_spec=pltpu.PrefetchScalarGridSpec(
            num_scalar_prefetch=1,
            grid=(tiles // many,),
            in_specs=[pl.BlockSpec((many, width, width), lambda i, rows: (i, 0, 0))],
            out_specs=[
                pl.BlockSpec((many, width, width), lambda i, rows: (i, 0, 0)),
                pl.BlockSpec((blocks, 8, width), lambda i, rows: (0, 0, 0)),
            ],
            scratch_shapes=[pltpu.VMEM((blocks, 8, width), F32)],
        ),
        compiler_params=params(8),
        cost_estimate=cost(2 * tiles * 8 * width * width, 6 * tiles * width * width),
        name="masks",
    )(tile_rows, edge_masks)

    agg = pl.pallas_call(
        forward_kernel,
        out_shape=shape((feats, nodes), BF16),
        in_specs=[SM, SM, VM, VM, VM, VM],
        out_specs=VM,
        scratch_shapes=[pltpu.VMEM((blocks, feats, width), F32)],
        compiler_params=params(12),
        cost_estimate=cost(2 * tiles * feats * width * width, 2 * tiles * (feats + width) * width),
        name="forward",
    )(slot, tile_rows, got, mask, embed, root)

    agg_full = lax.all_gather(agg, "feat", axis=0, tiled=True)
    part = lax.axis_index("feat").astype(jnp.int32).reshape(1)
    out, grad, scaled, terms = pl.pallas_call(
        dense_kernel,
        out_shape=(
            shape((feats, nodes), BF16),
            shape((feats, nodes), F32),
            shape((blocks, feats, width), BF16),
            shape((feats, hidden), F32),
        ),
        in_specs=[SM, VM, VM, VM, VM, VM],
        out_specs=(VM, VM, VM, VM),
        scratch_shapes=[pltpu.VMEM((hidden, 2 * width), F32)],
        compiler_params=params(16),
        cost_estimate=cost(
            2 * hidden * (hidden + 2 * feats) * nodes, 2 * hidden * nodes * 3, hidden * nodes
        ),
        name="dense",
    )(part, agg_full, agg, full, weight, root)

    rows = swap(terms.reshape(n_dom, feats // n_dom, hidden))
    send_back = pl.pallas_call(
        backward_kernel,
        out_shape=shape((2 * n_dom, feats, width), BF16),
        in_specs=[SM, SM, VM, VM],
        out_specs=VM,
        compiler_params=params(12),
        cost_estimate=cost(2 * tiles * feats * width * width, 2 * tiles * (feats + width) * width),
        name="backward",
    )(slot, tile_rows, scaled, mask)
    got_back = swap(send_back)

    row = jnp.sum(rows, axis=0, keepdims=True) / math.sqrt(nodes * n_dom)
    weight_grad = swap(jnp.broadcast_to(row, (n_dom,) + row.shape[1:])).reshape(feats, hidden)

    embed_grad = pl.pallas_call(
        combine_kernel,
        out_shape=shape((feats, nodes), F32),
        in_specs=[SM, VM, VM],
        out_specs=VM,
        scratch_shapes=[pltpu.VMEM((blocks, feats, width), F32)],
        compiler_params=params(8),
        cost_estimate=cost(2 * n_dom * feats * width, 4 * n_dom * feats * width),
        name="combine",
    )(want, got_back, grad)
    return (out, embed_grad, weight_grad)


def solution(mesh):
    in_specs = (
        P("feat", "dom"),
        P("feat", None),
        P("feat", "dom"),
        P("dom", None, None),
        P("dom"),
        P("dom", None),
        P("dom"),
    )
    out_specs = (P("feat", "dom"), P("feat", "dom"), P("feat", None))
    return jax.shard_map(
        per_device, mesh=mesh, in_specs=in_specs, out_specs=out_specs, check_vma=False
    )
```

time: 1300 us -> 191 us (0.15)
  waiting for transfers between devices: 1210 us -> 84.3 us
  blocking collectives: 8.25 us -> 58.7 us
  other arithmetic: 23.9 us -> 0.11 us
  Pallas kernels: 0 us -> 19 us
  starting transfers between devices: 0.34 us -> 18.3 us
  local copies, waits for them, and re-layouts: 24.5 us -> 8.42 us
  matrix products: 13.8 us -> 0 us
  between operations: 13.9 us -> 0.76 us
    psum x1 -> x0, waiting for transfers between devices: 496 us -> none  [per_device(): weight_grad = lax.psum(weight_terms, 'dom') / math.sqrt(nodes_all)]
    reduce_scatter x2 -> x0, waiting for transfers between devices: 401 us -> none  [the longest x1 366 us: per_device(): lax.psum_scatter(empty.at[target].add(partials, mode='drop'), 'dom', scat...]
    all_gather x1 -> x0, waiting for transfers between devices: 311 us -> none  [per_device(): gathered = lax.all_gather(embed, 'dom', axis=1, tiled=True)]
    all_to_all x0 -> x3, waiting for transfers between devices: none -> 84.3 us  [the longest x1 48.1 us: per_device(): got_back = swap(send_back)]
    all_to_all x0 -> x2, blocking collectives: none -> 38.7 us  [the longest x1 22.1 us: per_device(): want = swap(ask)]
    pallas_call x0 -> x7, Pallas kernels: none -> 19 us  [the longest x1 5.15 us: per_device(): pl.pallas_call(forward_kernel, out_shape=shape((feats, nodes), BF16), in_...]
    all_to_all x0 -> x3, starting transfers between devices: none -> 18.3 us  [the longest x1 6.5 us: per_device(): got = swap(send)]
    dot_general x7 -> x0, matrix products: 13.8 us -> none  [the longest x1 5 us: per_device(): jnp.einsum('ftj,tij->fti', fetched, mask_bf, preferred_element_type=jnp.f...]
  transfers between devices with their start and end apart: 4 -> 3, of which waited for: 4 -> 3; matrix products, arithmetic and copies ran while one was open for 3% -> 0% of each run, Pallas kernels for 0% -> 3%
where the time goes in v1:
time: 191 us; the launch traced here: 190 us
  waiting for transfers between devices  84.3 us (44%)
  blocking collectives  58.7 us (31%)
  Pallas kernels  19 us (10%)
  starting transfers between devices  18.3 us (10%)
  local copies, waits for them, and re-layouts  8.42 us (4%)
    all_to_all x1, waiting for transfers between devices, per_device(): got_back = swap(send_back)  48.1 us
    all_to_all x1, waiting for transfers between devices, per_device(): got = swap(send)  31.1 us
    all_to_all x1, blocking collectives, per_device(): want = swap(ask)  22.1 us
    all_to_all x1, blocking collectives, per_device(): rows = swap(terms.reshape(n_dom, feats // n_dom, hidden))  16.5 us
    all_gather x1, blocking collectives, per_device(): lax.all_gather(jnp.concatenate([cotangent, weight], axis=1), 'feat', axis...  12 us
    all_gather x1, blocking collectives, per_device(): agg_full = lax.all_gather(agg, 'feat', axis=0, tiled=True)  8.02 us
    unnamed x25, local copies, waits for them, and re-layouts  7.68 us
    all_to_all x1, starting transfers between devices, per_device(): got = swap(send)  6.5 us
  transfers between devices with their start and end apart: 3, of which 3 were waited for; matrix products, arithmetic and copies ran while one was open for 0% of the time, Pallas kernels for 3%

profile of v1, /device:TPU:8, one launch (start us, length us, event | category | flops | bytes accessed | tf_op | source)
XLA Modules:
  0.0 189.5 jit_solution(6536120580986412710)
XLA Ops:
  0.6 0.0 copy-start.9
  0.6 0.6 copy-done.9
  1.3 0.7 copy-done.10
  1.9 0.2 slots.1
  2.2 22.1 %all_to_all.31 = s32[64,1,128]{2,1,0:T(1,128)S(1)} all-to-all(s32[64,1,128]{2,1,0:T(1,128)S(1)} %bitcast.15), channel_id=1, replica_groups=mesh['dom'=64,'feat'=4] {'dom'}, dimensions={0} | all-to-all | bytes 65536 | tf_op jit(solution)/shard_map/all_to_all | solution.py:197
  24.3 0.9 copy-done.3
  25.2 3.0 %select.1 = bf16[128,64,128]{2,1,0:T(8,128)(2,1)} custom-call(s32[64,128]{1,0:T(8,128)S(1)} %bitcast.12, bf16[64,1024]{1,0:T(8,128)(2,1)S(1)} %copy-done.3), custom_call_target="tpu_custom_call" | custom-call | bytes 4194304 | tf_op jit(solution)/shard_map/select/pallas_call | solution.py:199
  28.2 6.5 %all-to-all-start.1 = ((bf16[128,64,128]{2,1,0:T(8,128)(2,1)}), bf16[128,64,128]{2,1,0:T(8,128)(2,1)}, u32[]{:S(2)}, u32[]{:S(2)}) async-start(bf16[128,64,128]{2,1,0:T(8,128)(2,1)} %select.1), calls=%async_computation.1 | async-start | bytes 4194304 | tf_op jit(solution)/shard_map/all_to_all | solution.py:208
  34.7 0.0 copy-done.8
  34.7 0.0 copy-start.1
  34.7 2.8 %copy-done.1 = s32[96,128,128]{2,1,0:T(8,128)S(1)} copy-done((s32[96,128,128]{2,1,0:T(8,128)S(1)}, s32[96,128,128]{2,1,0:T(8,128)}, u32[]{:S(2)}) %copy-start.1) | copy-done | bytes 6291480
  37.5 3.2 %masks.1 = (bf16[96,128,128]{2,1,0:T(8,128)(2,1)S(1)}, f32[8,8,128]{2,1,0:T(8,128)S(1)}) custom-call(s32[96]{0:T(128)S(1)} %copy-done.8, s32[96,128,128]{2,1,0:T(8,128)S(1)} %copy-done.1), custom_call_target="tpu_custom_call" | custom-call | flops 25165824 | bytes 9437184 | tf_op jit(solution)/shard_map/masks/pallas_call | solution.py:212
  40.7 12.0 %all_gather.7.full_ref = bf16[256,1280]{1,0:T(8,128)(2,1)} all-gather(bf16[64,1280]{1,0:T(8,128)(2,1)S(1)} %pad_maximum_fusion), channel_id=1, replica_groups=mesh['dom'=64,'feat'=4] {'feat'}, dimensions={0}, use_global_device_ids=true | all-gather | bytes 819200 | tf_op jit(solution)/shard_map/all_gather | solution.py:210
  52.7 31.1 %all-to-all-done.1.got_ref = bf16[128,64,128]{2,1,0:T(8,128)(2,1)} async-done(((bf16[128,64,128]{2,1,0:T(8,128)(2,1)}), bf16[128,64,128]{2,1,0:T(8,128)(2,1)}, u32[]{:S(2)}, u32[]{:S(2)}) %all-to-all-start.1) | async-done | bytes 2097184 | tf_op jit(solution)/shard_map/all_to_all | solution.py:208
  83.8 0.0 copy-done.4
  83.8 5.1 %forward.1.aggown_ref = bf16[64,1024]{1,0:T(8,128)(2,1)S(1)} custom-call(s32[96]{0:T(128)S(1)} %bitcast.16, s32[96]{0:T(128)S(1)} %copy-done.8, bf16[128,64,128]{2,1,0:T(8,128)(2,1)} %all-to-all-done.1.got_ref, bf16[96,128,128]{2,1,0:T(8,128)(2,1)S(1)} %get-tuple-element.13.mask_ref, bf16[64,1024]{1,0:T(8,128)(2,1)S(1)} %copy-done.4, ...), custom_call_target="tpu_custom_call" | custom-call | flops 201326592 | bytes 4718592 | tf_op jit(solution)/shard_map/forward/pallas_call | solution.py:230
  88.9 8.0 %all_gather.6.agg_ref = bf16[256,1024]{1,0:T(8,128)(2,1)S(1)} all-gather(bf16[64,1024]{1,0:T(8,128)(2,1)S(1)} %forward.1.aggown_ref), channel_id=1, replica_groups=mesh['dom'=64,'feat'=4] {'feat'}, dimensions={0}, use_global_device_ids=true | all-gather | bytes 655360 | tf_op jit(solution)/shard_map/all_gather | solution.py:241
  97.0 1.7 dense.1
  98.6 0.7 copy-done.5
  99.3 0.1 copy.11
  99.4 16.5 %all_to_all.32 = f32[64,1,256]{2,1,0:T(1,128)S(1)} all-to-all(f32[64,1,256]{2,1,0:T(1,128)S(1)} %copy.11), channel_id=1, replica_groups=mesh['dom'=64,'feat'=4] {'dom'}, dimensions={0} | all-to-all | bytes 131072 | tf_op jit(solution)/shard_map/all_to_all | solution.py:261
  115.9 0.1 reduce_sum.9
  116.0 0.7 broadcast_in_dim.2
  116.7 5.4 %all-to-all-start.4 = ((f32[64,1,256]{2,1,0:T(1,128)}), f32[64,1,256]{2,1,0:T(1,128)S(1)}, u32[]{:S(2)}, u32[]{:S(2)}) async-start(f32[64,1,256]{2,1,0:T(1,128)} %broadcast_in_dim.2), calls=%async_computation.4 | async-start | bytes 131072 | tf_op jit(solution)/shard_map/all_to_all | solution.py:274
  122.1 3.3 %backward.1 = bf16[128,64,128]{2,1,0:T(8,128)(2,1)S(1)} custom-call(s32[96]{0:T(128)S(1)} %bitcast.17, s32[96]{0:T(128)S(1)} %copy-done.8, bf16[8,64,128]{2,1,0:T(8,128)(2,1)S(1)} %get-tuple-element.16.scaled_ref, bf16[96,128,128]{2,1,0:T(8,128)(2,1)S(1)} %get-tuple-element.13.mask_ref), custom_call_target="tpu_custom_call" | custom-call | flops 201326592 | bytes 4718592 | tf_op jit(solution)/shard_map/backward/pallas_call | solution.py:262
  125.4 1.3 copy-done
  126.8 5.1 %all-to-all-done.4 = f32[64,1,256]{2,1,0:T(1,128)S(1)} async-done(((f32[64,1,256]{2,1,0:T(1,128)}), f32[64,1,256]{2,1,0:T(1,128)S(1)}, u32[]{:S(2)}, u32[]{:S(2)}) %all-to-all-start.4) | async-done | bytes 65568 | tf_op jit(solution)/shard_map/all_to_all | solution.py:274
  131.9 6.4 %all-to-all-start.2 = ((bf16[128,64,128]{2,1,0:T(8,128)(2,1)}), bf16[128,64,128]{2,1,0:T(8,128)(2,1)S(1)}, u32[]{:S(2)}, u32[]{:S(2)}) async-start(bf16[128,64,128]{2,1,0:T(8,128)(2,1)} %copy-done), calls=%async_computation.2 | async-start | bytes 4194304 | tf_op jit(solution)/shard_map/all_to_all | solution.py:271
  138.3 0.6 copy.14
  138.9 48.1 %all-to-all-done.2.got_ref = bf16[128,64,128]{2,1,0:T(8,128)(2,1)S(1)} async-done(((bf16[128,64,128]{2,1,0:T(8,128)(2,1)}), bf16[128,64,128]{2,1,0:T(8,128)(2,1)S(1)}, u32[]{:S(2)}, u32[]{:S(2)}) %all-to-all-start.2) | async-done | bytes 2097184 | tf_op jit(solution)/shard_map/all_to_all | solution.py:271
  187.0 0.0 copy-done.6
  187.0 2.5 %combine.1 = f32[64,1024]{1,0:T(8,128)} custom-call(s32[64,128]{1,0:T(8,128)S(1)} %bitcast.13, bf16[128,64,128]{2,1,0:T(8,128)(2,1)S(1)} %all-to-all-done.2.got_ref, f32[64,1024]{1,0:T(8,128)S(1)} %copy-done.6), custom_call_target="tpu_custom_call" | custom-call | flops 1048576 | bytes 2097152 | tf_op jit(solution)/shard_map/combine/pallas_call | solution.py:276
  (15 shorter events, 0.0 us)
Async XLA Ops:
  0.6 0.7 copy-start.9
  1.3 0.7 copy-start.10
  24.3 0.9 copy-start.3
  28.2 6.5 %copy-start.8 = (s32[96]{0:T(128)S(1)}, s32[96]{0:T(128)}, u32[]{:S(2)}) copy-start(s32[96]{0:T(128)} %rows_ref.5) | copy-start | bytes 1156
  28.2 55.6 %all-to-all-start.1 = ((bf16[128,64,128]{2,1,0:T(8,128)(2,1)}), bf16[128,64,128]{2,1,0:T(8,128)(2,1)}, u32[]{:S(2)}, u32[]{:S(2)}) async-start(bf16[128,64,128]{2,1,0:T(8,128)(2,1)} %select.1), calls=%async_computation.1 | async-start | bytes 4194304 | tf_op jit(solution)/shard_map/all_to_all | solution.py:208
  34.7 2.8 %copy-start.1 = (s32[96,128,128]{2,1,0:T(8,128)S(1)}, s32[96,128,128]{2,1,0:T(8,128)}, u32[]{:S(2)}) copy-start(s32[96,128,128]{2,1,0:T(8,128)} %edge_ref.1) | copy-start | bytes 18874372
  37.5 3.2 %copy-start.7 = (bf16[64,256]{1,0:T(8,128)(2,1)S(1)}, bf16[64,256]{1,0:T(8,128)(2,1)}, u32[]{:S(2)}) copy-start(bf16[64,256]{1,0:T(8,128)(2,1)} %weight_ref.1) | copy-start | bytes 98308
  37.5 3.2 %copy-start.11 = (bf16[64,1024]{1,0:T(8,128)(2,1)S(1)}, bf16[64,1024]{1,0:T(8,128)(2,1)}, u32[]{:S(2)}) copy-start(bf16[64,1024]{1,0:T(8,128)(2,1)} %param.9) | copy-start | bytes 393220
  37.5 46.3 %copy-start.4 = (bf16[64,1024]{1,0:T(8,128)(2,1)S(1)}, bf16[64,1024]{1,0:T(8,128)(2,1)}, u32[]{:S(2)}) copy-start(bf16[64,1024]{1,0:T(8,128)(2,1)} %own_ref.3) | copy-start | bytes 393220
  83.8 13.2 %copy-start.2 = (bf16[256,1280]{1,0:T(8,128)(2,1)S(1)}, bf16[256,1280]{1,0:T(8,128)(2,1)}, u32[]{:S(2)}) copy-start(bf16[256,1280]{1,0:T(8,128)(2,1)} %all_gather.7.full_ref) | copy-start | bytes 1966084
  98.6 0.7 copy-start.5
  116.7 15.1 %all-to-all-start.4 = ((f32[64,1,256]{2,1,0:T(1,128)}), f32[64,1,256]{2,1,0:T(1,128)S(1)}, u32[]{:S(2)}, u32[]{:S(2)}) async-start(f32[64,1,256]{2,1,0:T(1,128)} %broadcast_in_dim.2), calls=%async_computation.4 | async-start | bytes 131072 | tf_op jit(solution)/shard_map/all_to_all | solution.py:274
  125.4 1.3 copy-start
  126.8 60.2 %copy-start.6 = (f32[64,1024]{1,0:T(8,128)S(1)}, f32[64,1024]{1,0:T(8,128)}, u32[]{:S(2)}) copy-start(f32[64,1024]{1,0:T(8,128)} %copy-done.5) | copy-start | bytes 786436
  131.9 55.2 %all-to-all-start.2 = ((bf16[128,64,128]{2,1,0:T(8,128)(2,1)}), bf16[128,64,128]{2,1,0:T(8,128)(2,1)S(1)}, u32[]{:S(2)}, u32[]{:S(2)}) async-start(bf16[128,64,128]{2,1,0:T(8,128)(2,1)} %copy-done), calls=%async_computation.2 | async-start | bytes 4194304 | tf_op jit(solution)/shard_map/all_to_all | solution.py:271

commit v2 on v1

v2 whole, which is shorter than its diff:
```python
import functools
import math

import jax
import jax.numpy as jnp
from jax import lax
from jax.experimental import pallas as pl
from jax.experimental.pallas import tpu as pltpu
from jax.sharding import Mesh, PartitionSpec as P

F32 = jnp.float32
BF16 = jnp.bfloat16
FEAT = "feat"
VM = pl.BlockSpec(memory_space=pltpu.VMEM)
SM = pl.BlockSpec(memory_space=pltpu.SMEM)


def params(mib):
    return pltpu.CompilerParams(vmem_limit_bytes=mib << 20)


def cost(flops, moved, exps=0):
    return pl.CostEstimate(flops=flops, bytes_accessed=moved, transcendentals=exps)


def slots_kernel(z_size, y_size, me_ref, owner_ref, across_ref, sub_ref, ask_ref, slot_ref):
    tiles = owner_ref.shape[0]

    def place(owner, before):
        y = owner % y_size
        z = (owner // y_size) % z_size
        x = owner // (y_size * z_size)
        return ((x * y_size + y) * z_size + z) * 2 + before

    down = lax.broadcasted_iota(jnp.int32, (tiles, tiles), 0)
    right = lax.broadcasted_iota(jnp.int32, (tiles, tiles), 1)
    same = owner_ref[...] == across_ref[...]
    before = jnp.sum((same & (right < down)).astype(jnp.int32), axis=1, keepdims=True)
    before_across = jnp.sum((same & (down < right)).astype(jnp.int32), axis=0, keepdims=True)
    slot_ref[...] = place(across_ref[...], before_across)
    lane = lax.broadcasted_iota(jnp.int32, (tiles, ask_ref.shape[1]), 1)
    asked = jnp.where(lane == place(owner_ref[...], before), sub_ref[...], 0)
    row = lax.broadcasted_iota(jnp.int32, ask_ref.shape, 0)
    ask_ref[...] = jnp.where(row == me_ref[0], jnp.sum(asked, axis=0, keepdims=True), 0)


def select_kernel(me_ref, want_ref, held_ref, send_ref):
    readers = want_ref.shape[0]
    owners = held_ref.shape[0]
    width = send_ref.shape[2]
    base = me_ref[0] * (2 * owners)

    def body(reader, carry):
        for z in range(owners):
            for k in range(2):
                start = pl.multiple_of(want_ref[reader, base + 2 * z + k] * width, width)
                send_ref[(reader * owners + z) * 2 + k] = held_ref[z, :, pl.ds(start, width)]
        return carry

    lax.fori_loop(0, readers, body, 0)


def masks_kernel(rows_ref, edge_ref, mask_ref, root_ref, degree_ref):
    step = pl.program_id(0)
    many = edge_ref.shape[0]

    @pl.when(step == 0)
    def _():
        degree_ref[...] = jnp.zeros_like(degree_ref)

    ones = jnp.ones((8, edge_ref.shape[2]), BF16)
    for j in range(many):
        mask = edge_ref[j].astype(F32).astype(BF16)
        mask_ref[j] = mask
        count = lax.dot_general(ones, mask, (((1,), (1,)), ((), ())), preferred_element_type=F32)
        row = rows_ref[step * many + j]
        degree_ref[row] = degree_ref[row] + count

    @pl.when(step == pl.num_programs(0) - 1)
    def _():
        root_ref[...] = 1.0 / jnp.sqrt(1.0 + degree_ref[...])


def forward_kernel(slot_ref, rows_ref, got_ref, mask_ref, own_ref, root_ref, agg_ref, acc_ref):
    tiles = mask_ref.shape[0]
    blocks, _, width = acc_ref.shape
    acc_ref[...] = jnp.zeros_like(acc_ref)
    group = 8

    def body(step, carry):
        terms = []
        for j in range(group):
            tile = step * group + j
            terms.append(
                lax.dot_general(
                    got_ref[slot_ref[tile]],
                    mask_ref[tile],
                    (((1,), (1,)), ((), ())),
                    preferred_element_type=F32,
                )
            )
        for j in range(group):
            row = rows_ref[step * group + j]
            acc_ref[row] = acc_ref[row] + terms[j]
        return carry

    lax.fori_loop(0, tiles // group, body, 0)
    for r in range(blocks):
        cols = slice(r * width, (r + 1) * width)
        agg_ref[:, cols] = (
            own_ref[:, cols].astype(F32) + acc_ref[r] * root_ref[r, 0:1, :]
        ).astype(BF16)


def dense_kernel(
    part_ref, agg_ref, aggown_ref, weight_ref, root_ref, *refs
):
    out_ref, grad_ref, scaled_ref, terms_ref, act_ref, full_ref = refs[-6:]
    parts = refs[:-6]
    nodes = agg_ref.shape[1]
    feats = weight_ref.shape[0]
    width = scaled_ref.shape[2]
    first = pl.multiple_of(part_ref[0] * feats, feats)
    for m, ref in enumerate(parts):
        start = pl.multiple_of((part_ref[0] ^ m) * feats, feats)
        full_ref[pl.ds(start, feats), :] = ref[...]
    chunk = 2 * width
    terms = jnp.zeros(terms_ref.shape, F32)
    for c in range(nodes // chunk):
        cols = slice(c * chunk, (c + 1) * chunk)
        pre = lax.dot_general(
            full_ref[:, nodes:], agg_ref[:, cols], (((0,), (0,)), ((), ())), preferred_element_type=F32
        )
        gate = jax.nn.sigmoid(pre)
        act_ref[...] = pre * gate
        out_ref[:, cols] = act_ref[pl.ds(first, feats), :].astype(BF16)
        grad_pre = (full_ref[:, cols].astype(F32) * gate * (1.0 + pre * (1.0 - gate))).astype(BF16)
        grad = jnp.dot(weight_ref[...], grad_pre, preferred_element_type=F32)
        grad_ref[:, cols] = grad
        terms = terms + lax.dot_general(
            aggown_ref[:, cols], grad_pre, (((1,), (1,)), ((), ())), preferred_element_type=F32
        )
        for k in range(2):
            r = 2 * c + k
            scaled_ref[r] = (grad[:, k * width:(k + 1) * width] * root_ref[r, 0:1, :]).astype(BF16)
    terms_ref[...] = terms


def backward_kernel(slot_ref, rows_ref, scaled_ref, mask_ref, send_ref):
    tiles = mask_ref.shape[0]
    group = 8
    send_ref[...] = jnp.zeros_like(send_ref)

    def body(step, carry):
        for j in range(group):
            tile = step * group + j
            send_ref[slot_ref[tile]] = jnp.dot(
                scaled_ref[rows_ref[tile]], mask_ref[tile], preferred_element_type=F32
            ).astype(BF16)
        return carry

    lax.fori_loop(0, tiles // group, body, 0)


def gather_kernel(me_ref, want_ref, got_ref, sum_ref, acc_ref):
    owners, blocks, _, width = acc_ref.shape
    readers = want_ref.shape[0]
    base = me_ref[0] * (2 * owners)
    acc_ref[...] = jnp.zeros_like(acc_ref)

    def body(reader, carry):
        for z in range(owners):
            for k in range(2):
                block = want_ref[reader, base + 2 * z + k]
                acc_ref[z, block] = acc_ref[z, block] + got_ref[(reader * owners + z) * 2 + k].astype(F32)
        return carry

    lax.fori_loop(0, readers, body, 0)
    for z in range(owners):
        for r in range(blocks):
            sum_ref[z, :, r * width:(r + 1) * width] = acc_ref[z, r].astype(BF16)


def combine_kernel(got_ref, grad_ref, out_ref):
    total = grad_ref[...]
    for z in range(got_ref.shape[0]):
        total = total + got_ref[z].astype(F32)
    out_ref[...] = total


def pairwise(value, axes):
    for name, size in axes:
        bit = 1
        while bit < size:
            value = value + lax.ppermute(value, name, [(i, i ^ bit) for i in range(size)])
            bit *= 2
    return value


def per_device(embed, weight, cotangent, edge_masks, tile_rows, tile_owner, tile_sub):
    feats, nodes = embed.shape
    tiles, width, _ = edge_masks.shape
    blocks = nodes // width
    n_x, n_z, n_y = (lax.axis_size(name) for name in ("x", "z", "y_lo"))
    plane = ("x", "y_lo")
    peers = n_x * n_y
    slots = peers * n_z * 2
    hidden = weight.shape[1]
    shape = jax.ShapeDtypeStruct
    swap = functools.partial(lax.all_to_all, split_axis=0, concat_axis=0, tiled=True)

    held = swap(jnp.broadcast_to(embed[None], (n_z, feats, nodes)), "z")
    me = (lax.axis_index("x") * n_y + lax.axis_index("y_lo")).astype(jnp.int32).reshape(1)
    ask, slot = pl.pallas_call(
        functools.partial(slots_kernel, n_z, n_y),
        out_shape=(shape((peers, slots), jnp.int32), shape((1, tiles), jnp.int32)),
        in_specs=[SM, VM, VM, VM],
        out_specs=(VM, VM),
        compiler_params=params(4),
        name="slots",
    )(me, tile_owner, tile_owner.reshape(1, tiles), tile_sub.reshape(tiles, 1))
    slot = slot.reshape(tiles)
    want = pairwise(ask, (("y_lo", n_y), ("x", n_x)))

    mine = jnp.concatenate([cotangent, weight], axis=1)
    n_feat = hidden // feats
    parts = [mine] + [
        lax.ppermute(mine, FEAT, [(i, i ^ m) for i in range(n_feat)]) for m in range(1, n_feat)
    ]
    many = math.gcd(tiles, 12)
    mask, root = pl.pallas_call(
        masks_kernel,
        out_shape=(shape(edge_masks.shape, BF16), shape((blocks, 8, width), F32)),
        grid_spec=pltpu.PrefetchScalarGridSpec(
            num_scalar_prefetch=1,
            grid=(tiles // many,),
            in_specs=[pl.BlockSpec((many, width, width), lambda i, rows: (i, 0, 0))],
            out_specs=[
                pl.BlockSpec((many, width, width), lambda i, rows: (i, 0, 0)),
                pl.BlockSpec((blocks, 8, width), lambda i, rows: (0, 0, 0)),
            ],
            scratch_shapes=[pltpu.VMEM((blocks, 8, width), F32)],
        ),
        compiler_params=params(8),
        cost_estimate=cost(2 * tiles * 8 * width * width, 6 * tiles * width * width),
        name="masks",
    )(tile_rows, edge_masks)

    part = lax.axis_index(FEAT).astype(jnp.int32).reshape(1)
    held, parts, part, mask, root = lax.optimization_barrier((held, parts, part, mask, root))
    send = pl.pallas_call(
        select_kernel,
        out_shape=shape((slots, feats, width), BF16),
        in_specs=[SM, SM, VM],
        out_specs=VM,
        compiler_params=params(8),
        cost_estimate=cost(0, 2 * slots * feats * width * 2),
        name="select",
    )(me, want, held)
    got = swap(send, plane)

    agg = pl.pallas_call(
        forward_kernel,
        out_shape=shape((feats, nodes), BF16),
        in_specs=[SM, SM, VM, VM, VM, VM],
        out_specs=VM,
        scratch_shapes=[pltpu.VMEM((blocks, feats, width), F32)],
        compiler_params=params(12),
        cost_estimate=cost(2 * tiles * feats * width * width, 2 * tiles * (feats + width) * width),
        name="forward",
    )(slot, tile_rows, got, mask, embed, root)

    agg_full = lax.all_gather(agg, FEAT, axis=0, tiled=True)
    out, grad, scaled, terms = pl.pallas_call(
        dense_kernel,
        out_shape=(
            shape((feats, nodes), BF16),
            shape((feats, nodes), F32),
            shape((blocks, feats, width), BF16),
            shape((feats, hidden), F32),
        ),
        in_specs=[SM] + [VM] * (4 + n_feat),
        out_specs=(VM, VM, VM, VM),
        scratch_shapes=[
            pltpu.VMEM((hidden, 2 * width), F32),
            pltpu.VMEM((hidden, nodes + hidden), BF16),
        ],
        compiler_params=params(16),
        cost_estimate=cost(
            2 * hidden * (hidden + 2 * feats) * nodes, 2 * hidden * nodes * 3, hidden * nodes
        ),
        name="dense",
    )(part, agg_full, agg, weight, root, *parts)

    send_back = pl.pallas_call(
        backward_kernel,
        out_shape=shape((slots, feats, width), BF16),
        in_specs=[SM, SM, VM, VM],
        out_specs=VM,
        compiler_params=params(12),
        cost_estimate=cost(2 * tiles * feats * width * width, 2 * tiles * (feats + width) * width),
        name="backward",
    )(slot, tile_rows, scaled, mask)
    got_back = swap(send_back, plane)

    terms = pairwise(terms, (("z", n_z),))
    got_back, terms = lax.optimization_barrier((got_back, terms))
    terms = pairwise(terms, (("y_lo", n_y), ("x", n_x)))
    weight_grad = terms / math.sqrt(nodes * n_x * n_z * n_y)

    sums = pl.pallas_call(
        gather_kernel,
        out_shape=shape((n_z, feats, nodes), BF16),
        in_specs=[SM, SM, VM],
        out_specs=VM,
        scratch_shapes=[pltpu.VMEM((n_z, blocks, feats, width), F32)],
        compiler_params=params(12),
        cost_estimate=cost(slots * feats * width, 4 * slots * feats * width),
        name="gather",
    )(me, want, got_back)
    got_sums = swap(sums, "z")
    embed_grad = pl.pallas_call(
        combine_kernel,
        out_shape=shape((feats, nodes), F32),
        in_specs=[VM, VM],
        out_specs=VM,
        compiler_params=params(8),
        cost_estimate=cost(n_z * feats * nodes, 2 * n_z * feats * nodes),
        name="combine",
    )(got_sums, grad)
    return (out, embed_grad, weight_grad)


def solution(mesh):
    n_dom, n_feat = mesh.devices.shape
    wide = Mesh(mesh.devices.reshape(n_dom // 16, 8, 2, n_feat), ("x", "z", "y_lo", FEAT))
    dom = ("x", "z", "y_lo")
    in_specs = (
        P(FEAT, dom),
        P(FEAT, None),
        P(FEAT, dom),
        P(dom, None, None),
        P(dom),
        P(dom, None),
        P(dom),
    )
    out_specs = (P(FEAT, dom), P(FEAT, dom), P(FEAT, None))
    return jax.shard_map(
        per_device, mesh=wide, in_specs=in_specs, out_specs=out_specs, check_vma=False
    )
```

time: 191 us -> 167 us (0.87)
  blocking collectives: 58.7 us -> 39.9 us
  waiting for transfers between devices: 84.3 us -> 71.4 us
  starting transfers between devices: 18.3 us -> 26.6 us
    all_to_all x3, waiting for transfers between devices: 84.3 us -> 30 us  [the longest x1 13 us: per_device(): got_sums = swap(sums, 'z')]
    ppermute x0 -> x12, waiting for transfers between devices: none -> 41.4 us  [the longest x9 41.4 us: pairwise(): lax.ppermute(value, name, [(i, i ^ bit) for i in range(size)])]
    all_gather x2 -> x1, blocking collectives: 20 us -> 8.02 us  [per_device(): agg_full = lax.all_gather(agg, FEAT, axis=0, tiled=True)]
    ppermute x0 -> x12, starting transfers between devices: none -> 9.68 us  [the longest x9 6.23 us: pairwise(): lax.ppermute(value, name, [(i, i ^ bit) for i in range(size)])]
    all_to_all x2 -> x1, blocking collectives: 38.7 us -> 31.9 us  [per_device(): got = swap(send, plane)]
    unnamed x25 -> x26, local copies, waits for them, and re-layouts: 7.68 us -> 5.62 us
    pallas_call x3 -> x4, Pallas kernels: 6.48 us -> 8.01 us  [the longest x1 3.27 us: per_device(): pl.pallas_call(backward_kernel, out_shape=shape((slots, feats, width), BF...]
  transfers between devices with their start and end apart: 3 -> 15, of which waited for: 3 -> 11; matrix products, arithmetic and copies ran while one was open for 0% -> 1% of each run, Pallas kernels for 3% -> 2%
where the time goes in v2:
time: 167 us
  waiting for transfers between devices  71.4 us (43%)
  blocking collectives  39.9 us (24%)
  starting transfers between devices  26.6 us (16%)
  Pallas kernels  18.7 us (11%)
  local copies, waits for them, and re-layouts  7.81 us (5%)
    ppermute x9, waiting for transfers between devices, pairwise(): lax.ppermute(value, name, [(i, i ^ bit) for i in range(size)])  41.4 us
    all_to_all x1, blocking collectives, per_device(): got = swap(send, plane)  31.9 us
    all_to_all x1, waiting for transfers between devices, per_device(): got_sums = swap(sums, 'z')  13 us
    all_to_all x1, waiting for transfers between devices, per_device(): got_back = swap(send_back, plane)  12.8 us
    all_to_all x1, starting transfers between devices, per_device(): held = swap(jnp.broadcast_to(embed[None], (n_z, feats, nodes)), 'z')  8.47 us
    all_gather x1, blocking collectives, per_device(): agg_full = lax.all_gather(agg, FEAT, axis=0, tiled=True)  8.02 us
    ppermute x9, starting transfers between devices, pairwise(): lax.ppermute(value, name, [(i, i ^ bit) for i in range(size)])  6.23 us
    unnamed x26, local copies, waits for them, and re-layouts  5.62 us
  transfers between devices with their start and end apart: 15, of which 11 were waited for; matrix products, arithmetic and copies ran while one was open for 1% of the time, Pallas kernels for 2%

profile of v2, /device:TPU:8, one launch (start us, length us, event | category | flops | bytes accessed | tf_op | source)
XLA Modules:
  0.0 166.7 jit_solution(15940132580806847422)
XLA Ops:
  0.7 2.1 %broadcast_in_dim.2 = bf16[8,64,1024]{2,1,0:T(8,128)(2,1)} broadcast(bf16[64,1024]{1,0:T(8,128)(2,1)} %own_ref.1), dimensions={1,2} | broadcast | bytes 1179648 | tf_op jit(solution)/shard_map/broadcast_in_dim | solution.py:212
  2.8 8.5 %all-to-all-start = ((bf16[8,64,1024]{2,1,0:T(8,128)(2,1)}), bf16[8,64,1024]{2,1,0:T(8,128)(2,1)}, u32[]{:S(2)}, u32[]{:S(2)}) async-start(bf16[8,64,1024]{2,1,0:T(8,128)(2,1)} %broadcast_in_dim.2), calls=%async_computation | async-start | bytes 2097152 | tf_op jit(solution)/shard_map/all_to_all | solution.py:212
  11.3 1.5 collective-permute-start.2
  12.8 1.2 collective-permute-start.1
  15.7 6.8 %collective-permute-done.3 = s32[8,128]{1,0:T(8,128)S(1)} collective-permute-done((s32[8,128]{1,0:T(8,128)S(1)}, s32[8,128]{1,0:T(8,128)S(1)}, u32[]{:S(2)}, u32[]{:S(2)}) %collective-permute-start.3) | collective-permute-done | bytes 4128 | tf_op jit(solution)/shard_map/ppermute | solution.py:195
  22.5 1.5 collective-permute-start.4
  24.0 2.1 %collective-permute-done.4 = s32[8,128]{1,0:T(8,128)S(1)} collective-permute-done((s32[8,128]{1,0:T(8,128)S(1)}, s32[8,128]{1,0:T(8,128)S(1)}, u32[]{:S(2)}, u32[]{:S(2)}) %collective-permute-start.4) | collective-permute-done | bytes 4128 | tf_op jit(solution)/shard_map/ppermute | solution.py:195
  26.2 3.0 %collective-permute-start.5 = (s32[8,128]{1,0:T(8,128)S(1)}, s32[8,128]{1,0:T(8,128)}, u32[]{:S(2)}, u32[]{:S(2)}) collective-permute-start(s32[8,128]{1,0:T(8,128)S(1)} %add.32), channel_id=1, source_target_pairs={{0,128},{64,192},{128,0},{192,64},{1,129},{65,193},{129,1},{193,65... | collective-permute-start | bytes 12296 | tf_op jit(solution)/shard_map/ppermute | solution.py:195
  29.2 2.8 %copy-done.1 = s32[96,128,128]{2,1,0:T(8,128)S(1)} copy-done((s32[96,128,128]{2,1,0:T(8,128)S(1)}, s32[96,128,128]{2,1,0:T(8,128)}, u32[]{:S(2)}) %copy-start.1) | copy-done | bytes 6291480
  32.0 3.2 %masks.1 = (bf16[96,128,128]{2,1,0:T(8,128)(2,1)S(1)}, f32[8,8,128]{2,1,0:T(8,128)S(1)}) custom-call(s32[96]{0:T(128)S(1)} %copy-done.8, s32[96,128,128]{2,1,0:T(8,128)S(1)} %copy-done.1), custom_call_target="tpu_custom_call" | custom-call | flops 25165824 | bytes 9437184 | tf_op jit(solution)/shard_map/masks/pallas_call | solution.py:231
  35.9 4.2 %all-to-all-done.held_ref = bf16[8,64,1024]{2,1,0:T(8,128)(2,1)} async-done(((bf16[8,64,1024]{2,1,0:T(8,128)(2,1)}), bf16[8,64,1024]{2,1,0:T(8,128)(2,1)}, u32[]{:S(2)}, u32[]{:S(2)}) %all-to-all-start) | async-done | bytes 1048608 | tf_op jit(solution)/shard_map/all_to_all | solution.py:212
  40.1 1.8 %select.1 = bf16[128,64,128]{2,1,0:T(8,128)(2,1)S(1)} custom-call(s32[1]{0:T(128)} %bitcast.1.me_ref, s32[8,128]{1,0:T(8,128)S(1)} %add.33.want_ref, bf16[8,64,1024]{2,1,0:T(8,128)(2,1)} %all-to-all-done.held_ref), custom_call_target="tpu_custom_call" | custom-call | bytes 4194304 | tf_op jit(solution)/shard_map/select/pallas_call | solution.py:251
  41.9 31.9 %all_to_all.20.got_ref = bf16[128,64,128]{2,1,0:T(8,128)(2,1)S(1)} all-to-all(bf16[128,64,128]{2,1,0:T(8,128)(2,1)S(1)} %select.1), channel_id=1, replica_groups=mesh['x'=4,'z'=8,'y_lo'=2,'feat'=4] {'x','y_lo'}, dimensions={0} | all-to-all | bytes 4194304 | tf_op jit(solution)/shard_map/all_to_all | solution.py:260
  73.8 4.0 %forward.1.aggown_ref = bf16[64,1024]{1,0:T(8,128)(2,1)S(1)} custom-call(s32[96]{0:T(128)S(1)} %bitcast.6, s32[96]{0:T(128)S(1)} %copy-done.8, bf16[128,64,128]{2,1,0:T(8,128)(2,1)S(1)} %all_to_all.20.got_ref, bf16[96,128,128]{2,1,0:T(8,128)(2,1)S(1)} %get-tuple-element.27.mask_ref, bf16[64,1024]{1,0:T(8,128)(2,1)S(1)} %copy-done.2, ...), custom_call_target="tpu_custom_call" | custom-call | flops 201326592 | bytes 4718592 | tf_op jit(solution)/shard_map/forward/pallas_call | solution.py:262
  77.9 8.0 %all_gather.3.agg_ref = bf16[256,1024]{1,0:T(8,128)(2,1)S(1)} all-gather(bf16[64,1024]{1,0:T(8,128)(2,1)S(1)} %forward.1.aggown_ref), channel_id=1, replica_groups=mesh['x'=4,'z'=8,'y_lo'=2,'feat'=4] {'feat'}, dimensions={0}, use_global_device_ids=true | all-gather | bytes 655360 | tf_op jit(solution)/shard_map/all_gather | solution.py:273
  85.9 2.7 %dense.1 = (bf16[64,1024]{1,0:T(8,128)(2,1)}, f32[64,1024]{1,0:T(8,128)S(1)}, bf16[8,64,128]{2,1,0:T(8,128)(2,1)S(1)}, f32[64,256]{1,0:T(8,128)S(1)}) custom-call(s32[1]{0:T(128)} %bitcast.part_ref, bf16[256,1024]{1,0:T(8,128)(2,1)S(1)} %all_gather.3.agg_ref, bf16[64,1024]{1,0:T(8,128)(2,1)S(1)} %forward.1.aggown_ref, bf16[64,256]{1,0:T(8,128)(2,1)S(1)} %copy-done.5, ...), custom_call_target="tpu_custom_call" | custom-call | flops 201326592 | bytes 1572864 | tf_op jit(solution)/shard_map/dense/pallas_call | solution.py:274
  88.6 0.7 copy-done.3
  89.9 3.3 %backward.1 = bf16[128,64,128]{2,1,0:T(8,128)(2,1)S(1)} custom-call(s32[96]{0:T(128)S(1)} %bitcast.7, s32[96]{0:T(128)S(1)} %copy-done.8, bf16[8,64,128]{2,1,0:T(8,128)(2,1)S(1)} %get-tuple-element.34.scaled_ref, bf16[96,128,128]{2,1,0:T(8,128)(2,1)S(1)} %get-tuple-element.27.mask_ref), custom_call_target="tpu_custom_call" | custom-call | flops 201326592 | bytes 4718592 | tf_op jit(solution)/shard_map/backward/pallas_call | solution.py:295
  93.2 1.4 copy-done
  94.5 4.8 %all-to-all-start.2 = ((bf16[128,64,128]{2,1,0:T(8,128)(2,1)}), bf16[128,64,128]{2,1,0:T(8,128)(2,1)S(1)}, u32[]{:S(2)}, u32[]{:S(2)}) async-start(bf16[128,64,128]{2,1,0:T(8,128)(2,1)} %copy-done), calls=%async_computation.2 | async-start | bytes 4194304 | tf_op jit(solution)/shard_map/all_to_all | solution.py:304
  99.4 4.3 %collective-permute-done.6 = f32[64,256]{1,0:T(8,128)S(1)} collective-permute-done((f32[64,256]{1,0:T(8,128)S(1)}, f32[64,256]{1,0:T(8,128)S(1)}, u32[]{:S(2)}, u32[]{:S(2)}) %collective-permute-start.6) | collective-permute-done | bytes 65568 | tf_op jit(solution)/shard_map/ppermute | solution.py:195
  103.7 5.4 %collective-permute-done.7 = f32[64,256]{1,0:T(8,128)S(1)} collective-permute-done((f32[64,256]{1,0:T(8,128)S(1)}, f32[64,256]{1,0:T(8,128)S(1)}, u32[]{:S(2)}, u32[]{:S(2)}) %collective-permute-start.7) | collective-permute-done | bytes 65568 | tf_op jit(solution)/shard_map/ppermute | solution.py:195
  109.3 8.8 %collective-permute-done.8 = f32[64,256]{1,0:T(8,128)S(1)} collective-permute-done((f32[64,256]{1,0:T(8,128)S(1)}, f32[64,256]{1,0:T(8,128)S(1)}, u32[]{:S(2)}, u32[]{:S(2)}) %collective-permute-start.8) | collective-permute-done | bytes 65568 | tf_op jit(solution)/shard_map/ppermute | solution.py:195
  118.1 12.8 %all-to-all-done.2.got_ref = bf16[128,64,128]{2,1,0:T(8,128)(2,1)S(1)} async-done(((bf16[128,64,128]{2,1,0:T(8,128)(2,1)}), bf16[128,64,128]{2,1,0:T(8,128)(2,1)S(1)}, u32[]{:S(2)}, u32[]{:S(2)}) %all-to-all-start.2) | async-done | bytes 2097184 | tf_op jit(solution)/shard_map/all_to_all | solution.py:304
  130.9 2.7 %gather.1 = bf16[8,64,1024]{2,1,0:T(8,128)(2,1)} custom-call(s32[1]{0:T(128)} %bitcast.1.me_ref, s32[8,128]{1,0:T(8,128)S(1)} %add.33.want_ref, bf16[128,64,128]{2,1,0:T(8,128)(2,1)S(1)} %all-to-all-done.2.got_ref), custom_call_target="tpu_custom_call" | custom-call | flops 1048576 | bytes 4194304 | tf_op jit(solution)/shard_map/gather/pallas_call | solution.py:311
  133.5 3.7 %all-to-all-start.3 = ((bf16[8,64,1024]{2,1,0:T(8,128)(2,1)}), bf16[8,64,1024]{2,1,0:T(8,128)(2,1)S(1)}, u32[]{:S(2)}, u32[]{:S(2)}) async-start(bf16[8,64,1024]{2,1,0:T(8,128)(2,1)} %gather.1), calls=%async_computation.3 | async-start | bytes 2097152 | tf_op jit(solution)/shard_map/all_to_all | solution.py:321
  137.2 0.8 collective-permute-start.9
  138.0 3.5 %collective-permute-done.9 = f32[64,256]{1,0:T(8,128)S(1)} collective-permute-done((f32[64,256]{1,0:T(8,128)S(1)}, f32[64,256]{1,0:T(8,128)S(1)}, u32[]{:S(2)}, u32[]{:S(2)}) %collective-permute-start.9) | collective-permute-done | bytes 65568 | tf_op jit(solution)/shard_map/ppermute | solution.py:195
  141.7 4.7 %collective-permute-done.10 = f32[64,256]{1,0:T(8,128)S(1)} collective-permute-done((f32[64,256]{1,0:T(8,128)S(1)}, f32[64,256]{1,0:T(8,128)S(1)}, u32[]{:S(2)}, u32[]{:S(2)}) %collective-permute-start.10) | collective-permute-done | bytes 65568 | tf_op jit(solution)/shard_map/ppermute | solution.py:195
  146.5 5.8 %collective-permute-done.11 = f32[64,256]{1,0:T(8,128)S(1)} collective-permute-done((f32[64,256]{1,0:T(8,128)S(1)}, f32[64,256]{1,0:T(8,128)S(1)}, u32[]{:S(2)}, u32[]{:S(2)}) %collective-permute-start.11) | collective-permute-done | bytes 65568 | tf_op jit(solution)/shard_map/ppermute | solution.py:195
  152.9 13.0 %all-to-all-done.3.got_ref = bf16[8,64,1024]{2,1,0:T(8,128)(2,1)S(1)} async-done(((bf16[8,64,1024]{2,1,0:T(8,128)(2,1)}), bf16[8,64,1024]{2,1,0:T(8,128)(2,1)S(1)}, u32[]{:S(2)}, u32[]{:S(2)}) %all-to-all-start.3) | async-done | bytes 1048608 | tf_op jit(solution)/shard_map/all_to_all | solution.py:321
  165.9 0.8 combine.1
  (46 shorter events, 4.1 us)
Async XLA Ops:
  0.6 10.6 %copy-start.10 = (bf16[64,1024]{1,0:T(8,128)(2,1)S(1)}, bf16[64,1024]{1,0:T(8,128)(2,1)}, u32[]{:S(2)}) copy-start(bf16[64,1024]{1,0:T(8,128)(2,1)} %param.9) | copy-start | bytes 393220
  0.6 10.6 %copy-start.5 = (bf16[64,256]{1,0:T(8,128)(2,1)S(1)}, bf16[64,256]{1,0:T(8,128)(2,1)}, u32[]{:S(2)}) copy-start(bf16[64,256]{1,0:T(8,128)(2,1)} %weight_ref.1) | copy-start | bytes 98308
  0.7 14.1 %copy-start.11 = (s32[96]{0:T(128)S(1)}, s32[96]{0:T(128)}, u32[]{:S(2)}) copy-start(s32[96]{0:T(128)} %param.13) | copy-start | bytes 1156
  0.7 14.2 %copy-start.9 = (s32[96,1]{0,1:T(1,128)S(1)}, s32[96,1]{0,1:T(1,128)}, u32[]{:S(2)}) copy-start(s32[96,1]{0,1:T(1,128)} %param.12) | copy-start | bytes 1156
  0.7 28.5 %copy-start.8 = (s32[96]{0:T(128)S(1)}, s32[96]{0:T(128)}, u32[]{:S(2)}) copy-start(s32[96]{0:T(128)} %rows_ref.5) | copy-start | bytes 1156
  2.8 37.3 %all-to-all-start = ((bf16[8,64,1024]{2,1,0:T(8,128)(2,1)}), bf16[8,64,1024]{2,1,0:T(8,128)(2,1)}, u32[]{:S(2)}, u32[]{:S(2)}) async-start(bf16[8,64,1024]{2,1,0:T(8,128)(2,1)} %broadcast_in_dim.2), calls=%async_computation | async-start | bytes 2097152 | tf_op jit(solution)/shard_map/all_to_all | solution.py:212
  11.3 24.6 %collective-permute-start.2 = (bf16[64,1280]{1,0:T(8,128)(2,1)S(1)}, bf16[64,1280]{1,0:T(8,128)(2,1)S(1)}, u32[]{:S(2)}, u32[]{:S(2)}) collective-permute-start(bf16[64,1280]{1,0:T(8,128)(2,1)S(1)} %constant_dynamic-update-slice_fusion.refs_0_), channel_id=1, source_target_pairs={{0,3},{1,2},{2,1},{3,0},{4,7},{5,6},{6,5},{7,4},{8,11},{9,10},{10,... | collective-permute-start | bytes 491528 | tf_op jit(solution)/shard_map/ppermute | solution.py:228
  12.8 23.0 %collective-permute-start.1 = (bf16[64,1280]{1,0:T(8,128)(2,1)S(1)}, bf16[64,1280]{1,0:T(8,128)(2,1)}, u32[]{:S(2)}, u32[]{:S(2)}) collective-permute-start(bf16[64,1280]{1,0:T(8,128)(2,1)S(1)} %constant_dynamic-update-slice_fusion.refs_0_), channel_id=1, source_target_pairs={{0,2},{1,3},{2,0},{3,1},{4,6},{5,7},{6,4},{7,5},{8,10},{9,11},{10,... | collective-permute-start | bytes 491528 | tf_op jit(solution)/shard_map/ppermute | solution.py:228
  14.1 21.8 %collective-permute-start = (bf16[64,1280]{1,0:T(8,128)(2,1)S(1)}, bf16[64,1280]{1,0:T(8,128)(2,1)}, u32[]{:S(2)}, u32[]{:S(2)}) collective-permute-start(bf16[64,1280]{1,0:T(8,128)(2,1)S(1)} %constant_dynamic-update-slice_fusion.refs_0_), channel_id=1, source_target_pairs={{0,1},{1,0},{2,3},{3,2},{4,5},{5,4},{6,7},{7,6},{8,9},{9,8},{10,11... | collective-permute-start | bytes 491528 | tf_op jit(solution)/shard_map/ppermute | solution.py:228
  15.2 7.3 %collective-permute-start.3 = (s32[8,128]{1,0:T(8,128)S(1)}, s32[8,128]{1,0:T(8,128)S(1)}, u32[]{:S(2)}, u32[]{:S(2)}) collective-permute-start(s32[8,128]{1,0:T(8,128)S(1)} %get-tuple-element.25), channel_id=1, source_target_pairs={{0,4},{4,0},{1,5},{5,1},{2,6},{6,2},{3,7},{7,3},{8,12},{12,8},{9,1... | collective-permute-start | bytes 12296 | tf_op jit(solution)/shard_map/ppermute | solution.py:195
  22.5 3.6 %collective-permute-start.4 = (s32[8,128]{1,0:T(8,128)S(1)}, s32[8,128]{1,0:T(8,128)S(1)}, u32[]{:S(2)}, u32[]{:S(2)}) collective-permute-start(s32[8,128]{1,0:T(8,128)S(1)} %add.31), channel_id=1, source_target_pairs={{0,64},{64,0},{128,192},{192,128},{1,65},{65,1},{129,193},{193,129... | collective-permute-start | bytes 12296 | tf_op jit(solution)/shard_map/ppermute | solution.py:195
  26.2 9.0 %collective-permute-start.5 = (s32[8,128]{1,0:T(8,128)S(1)}, s32[8,128]{1,0:T(8,128)}, u32[]{:S(2)}, u32[]{:S(2)}) collective-permute-start(s32[8,128]{1,0:T(8,128)S(1)} %add.32), channel_id=1, source_target_pairs={{0,128},{64,192},{128,0},{192,64},{1,129},{65,193},{129,1},{193,65... | collective-permute-start | bytes 12296 | tf_op jit(solution)/shard_map/ppermute | solution.py:195
  29.2 2.8 %copy-start.1 = (s32[96,128,128]{2,1,0:T(8,128)S(1)}, s32[96,128,128]{2,1,0:T(8,128)}, u32[]{:S(2)}) copy-start(s32[96,128,128]{2,1,0:T(8,128)} %edge_ref.1) | copy-start | bytes 18874372
  41.9 31.9 %copy-start.2 = (bf16[64,1024]{1,0:T(8,128)(2,1)S(1)}, bf16[64,1024]{1,0:T(8,128)(2,1)}, u32[]{:S(2)}) copy-start(bf16[64,1024]{1,0:T(8,128)(2,1)} %own_ref.1) | copy-start | bytes 393220
  88.6 0.7 copy-start.3
  89.3 0.6 copy-start.6
  93.2 1.4 copy-start
  94.5 4.8 %copy-start.7 = (f32[64,256]{1,0:T(8,128)S(1)}, f32[64,256]{1,0:T(8,128)}, u32[]{:S(2)}) copy-start(f32[64,256]{1,0:T(8,128)} %copy-done.6) | copy-start | bytes 196612
  94.5 36.4 %all-to-all-start.2 = ((bf16[128,64,128]{2,1,0:T(8,128)(2,1)}), bf16[128,64,128]{2,1,0:T(8,128)(2,1)S(1)}, u32[]{:S(2)}, u32[]{:S(2)}) async-start(bf16[128,64,128]{2,1,0:T(8,128)(2,1)} %copy-done), calls=%async_computation.2 | async-start | bytes 4194304 | tf_op jit(solution)/shard_map/all_to_all | solution.py:304
  99.3 4.3 %collective-permute-start.6 = (f32[64,256]{1,0:T(8,128)S(1)}, f32[64,256]{1,0:T(8,128)S(1)}, u32[]{:S(2)}, u32[]{:S(2)}) collective-permute-start(f32[64,256]{1,0:T(8,128)S(1)} %copy-done.7), channel_id=1, source_target_pairs={{0,8},{8,0},{16,24},{24,16},{32,40},{40,32},{48,56},{56,48},{1,9},... | collective-permute-start | bytes 196616 | tf_op jit(solution)/shard_map/ppermute | solution.py:195
  103.6 5.5 %collective-permute-start.7 = (f32[64,256]{1,0:T(8,128)S(1)}, f32[64,256]{1,0:T(8,128)S(1)}, u32[]{:S(2)}, u32[]{:S(2)}) collective-permute-start(f32[64,256]{1,0:T(8,128)S(1)} %add.34), channel_id=1, source_target_pairs={{0,16},{8,24},{16,0},{24,8},{32,48},{40,56},{48,32},{56,40},{1,17}... | collective-permute-start | bytes 196616 | tf_op jit(solution)/shard_map/ppermute | solution.py:195
  109.2 8.9 %collective-permute-start.8 = (f32[64,256]{1,0:T(8,128)S(1)}, f32[64,256]{1,0:T(8,128)S(1)}, u32[]{:S(2)}, u32[]{:S(2)}) collective-permute-start(f32[64,256]{1,0:T(8,128)S(1)} %add.35), channel_id=1, source_target_pairs={{0,32},{8,40},{16,48},{24,56},{32,0},{40,8},{48,16},{56,24},{1,33}... | collective-permute-start | bytes 196616 | tf_op jit(solution)/shard_map/ppermute | solution.py:195
  133.5 32.3 %copy-start.4 = (f32[64,1024]{1,0:T(8,128)S(1)}, f32[64,1024]{1,0:T(8,128)}, u32[]{:S(2)}) copy-start(f32[64,1024]{1,0:T(8,128)} %copy-done.3) | copy-start | bytes 786436
  133.5 32.3 %all-to-all-start.3 = ((bf16[8,64,1024]{2,1,0:T(8,128)(2,1)}), bf16[8,64,1024]{2,1,0:T(8,128)(2,1)S(1)}, u32[]{:S(2)}, u32[]{:S(2)}) async-start(bf16[8,64,1024]{2,1,0:T(8,128)(2,1)} %gather.1), calls=%async_computation.3 | async-start | bytes 2097152 | tf_op jit(solution)/shard_map/all_to_all | solution.py:321
  137.2 4.4 %collective-permute-start.9 = (f32[64,256]{1,0:T(8,128)S(1)}, f32[64,256]{1,0:T(8,128)S(1)}, u32[]{:S(2)}, u32[]{:S(2)}) collective-permute-start(f32[64,256]{1,0:T(8,128)S(1)} %add.36), channel_id=1, source_target_pairs={{0,4},{4,0},{1,5},{5,1},{2,6},{6,2},{3,7},{7,3},{8,12},{12,8},{9,1... | collective-permute-start | bytes 196616 | tf_op jit(solution)/shard_map/ppermute | solution.py:195
  141.6 4.8 %collective-permute-start.10 = (f32[64,256]{1,0:T(8,128)S(1)}, f32[64,256]{1,0:T(8,128)S(1)}, u32[]{:S(2)}, u32[]{:S(2)}) collective-permute-start(f32[64,256]{1,0:T(8,128)S(1)} %add.37), channel_id=1, source_target_pairs={{0,64},{64,0},{128,192},{192,128},{1,65},{65,1},{129,193},{193,129... | collective-permute-start | bytes 196616 | tf_op jit(solution)/shard_map/ppermute | solution.py:195
  146.4 5.9 %collective-permute-start.11 = (f32[64,256]{1,0:T(8,128)S(1)}, f32[64,256]{1,0:T(8,128)S(1)}, u32[]{:S(2)}, u32[]{:S(2)}) collective-permute-start(f32[64,256]{1,0:T(8,128)S(1)} %add.38), channel_id=1, source_target_pairs={{0,128},{64,192},{128,0},{192,64},{1,129},{65,193},{129,1},{193,65... | collective-permute-start | bytes 196616 | tf_op jit(solution)/shard_map/ppermute | solution.py:195

commit v3 on v2

--- a/solution.py
+++ b/solution.py
@@ -146,24 +146,36 @@
     terms_ref[...] = terms
 
 
-def backward_kernel(slot_ref, rows_ref, scaled_ref, mask_ref, send_ref):
+def backward_kernel(slot_ref, rows_ref, scaled_ref, mask_ref, terms_ref, send_ref):
     tiles = mask_ref.shape[0]
+    feats, hidden = terms_ref.shape
+    width = send_ref.shape[2]
+    end = send_ref.shape[1] - feats * hidden // width
+    per_peer = end // feats
     group = 8
-    send_ref[...] = jnp.zeros_like(send_ref)
+    send_ref[:, :end, :] = jnp.zeros((send_ref.shape[0], end, width), BF16)
 
     def body(step, carry):
         for j in range(group):
             tile = step * group + j
-            send_ref[slot_ref[tile]] = jnp.dot(
+            slot = slot_ref[tile]
+            start = pl.multiple_of((slot % per_peer) * feats, feats)
+            send_ref[slot // per_peer, pl.ds(start, feats), :] = jnp.dot(
                 scaled_ref[rows_ref[tile]], mask_ref[tile], preferred_element_type=F32
             ).astype(BF16)
         return carry
 
     lax.fori_loop(0, tiles // group, body, 0)
-
-
-def gather_kernel(me_ref, want_ref, got_ref, sum_ref, acc_ref):
-    owners, blocks, _, width = acc_ref.shape
+    for h in range(hidden // width):
+        part = terms_ref[:, h * width:(h + 1) * width].astype(BF16)
+        for p in range(send_ref.shape[0]):
+            send_ref[p, end + h * feats:end + (h + 1) * feats, :] = part
+
+
+def gather_kernel(me_ref, want_ref, got_ref, up_ref, down_ref, *refs):
+    acc_ref = refs[-1]
+    sums = refs[:-1]
+    owners, blocks, feats, width = acc_ref.shape
     readers = want_ref.shape[0]
     base = me_ref[0] * (2 * owners)
     acc_ref[...] = jnp.zeros_like(acc_ref)
@@ -172,20 +184,58 @@
         for z in range(owners):
             for k in range(2):
                 block = want_ref[reader, base + 2 * z + k]
-                acc_ref[z, block] = acc_ref[z, block] + got_ref[(reader * owners + z) * 2 + k].astype(F32)
+                start = (2 * z + k) * feats
+                acc_ref[z, block] = acc_ref[z, block] + got_ref[reader, start:start + feats, :].astype(F32)
         return carry
 
     lax.fori_loop(0, readers, body, 0)
-    for z in range(owners):
+    end = 2 * owners * feats
+    low = up_ref.shape[0] - feats
+    for h in range((got_ref.shape[1] - end) // low):
+        rows = slice(end + h * low, end + (h + 1) * low)
+        terms = got_ref[0, rows, :].astype(F32)
+        for q in range(1, readers):
+            terms = terms + got_ref[q, rows, :].astype(F32)
+        up_ref[feats:, h * width:(h + 1) * width] = terms.astype(BF16)
+        down_ref[feats:, h * width:(h + 1) * width] = terms.astype(BF16)
+    half = owners // 2
+    for d in range(owners):
+        ref = up_ref if d == half else down_ref if d == half + 1 else sums[d - 2 * (d > half)]
+        z = (me_ref[1] + d) % owners
         for r in range(blocks):
-            sum_ref[z, :, r * width:(r + 1) * width] = acc_ref[z, r].astype(BF16)
-
-
-def combine_kernel(got_ref, grad_ref, out_ref):
-    total = grad_ref[...]
-    for z in range(got_ref.shape[0]):
-        total = total + got_ref[z].astype(F32)
-    out_ref[...] = total
+            ref[:feats, r * width:(r + 1) * width] = acc_ref[z, r].astype(ref.dtype)
+
+
+def hop_kernel(*refs):
+    many = len(refs) // 3
+    for got_ref, sum_ref, on_ref in zip(refs[:many], refs[many:2 * many], refs[2 * many:]):
+        feats = sum_ref.shape[0]
+        on_ref[:feats, :] = (got_ref[:feats, :].astype(F32) + sum_ref[...]).astype(BF16)
+        on_ref[feats:, :] = got_ref[feats:, :]
+
+
+def combine_kernel(scale, me_ref, grad_ref, own_ref, *refs):
+    out_ref, weight_ref, terms_ref = refs[-3:]
+    places = refs[:-3]
+    planes = len(places)
+    feats, hidden = weight_ref.shape
+    low, nodes = terms_ref.shape[1:]
+    half = planes // 2
+    out_ref[...] = grad_ref[...] + own_ref[...] + (
+        places[planes - half][:feats, :].astype(F32) + places[half - 1][:feats, :].astype(F32)
+    )
+    for d, ref in enumerate(places):
+        terms_ref[(me_ref[1] + d) % planes] = ref[feats:, :].astype(F32)
+    total = terms_ref[0]
+    for z in range(1, planes):
+        total = total + terms_ref[z]
+    total = total * scale
+    lanes = 128
+    per = feats // low
+    for h in range(hidden // lanes):
+        for g in range(per):
+            start = (h * per + g) * lanes
+            weight_ref[g * low:(g + 1) * low, h * lanes:(h + 1) * lanes] = total[:, start:start + lanes]
 
 
 def pairwise(value, axes):
@@ -210,7 +260,8 @@
     swap = functools.partial(lax.all_to_all, split_axis=0, concat_axis=0, tiled=True)
 
     held = swap(jnp.broadcast_to(embed[None], (n_z, feats, nodes)), "z")
-    me = (lax.axis_index("x") * n_y + lax.axis_index("y_lo")).astype(jnp.int32).reshape(1)
+    me = jnp.stack([lax.axis_index("x") * n_y + lax.axis_index("y_lo"), lax.axis_index("z")])
+    me = me.astype(jnp.int32)
     ask, slot = pl.pallas_call(
         functools.partial(slots_kernel, n_z, n_y),
         out_shape=(shape((peers, slots), jnp.int32), shape((1, tiles), jnp.int32)),
@@ -292,42 +343,71 @@
         name="dense",
     )(part, agg_full, agg, weight, root, *parts)
 
+    extra = feats * hidden // width
     send_back = pl.pallas_call(
         backward_kernel,
-        out_shape=shape((slots, feats, width), BF16),
-        in_specs=[SM, SM, VM, VM],
+        out_shape=shape((peers, 2 * n_z * feats + extra, width), BF16),
+        in_specs=[SM, SM, VM, VM, VM],
         out_specs=VM,
         compiler_params=params(12),
         cost_estimate=cost(2 * tiles * feats * width * width, 2 * tiles * (feats + width) * width),
         name="backward",
-    )(slot, tile_rows, scaled, mask)
+    )(slot, tile_rows, scaled, mask, terms)
     got_back = swap(send_back, plane)
 
-    terms = pairwise(terms, (("z", n_z),))
-    got_back, terms = lax.optimization_barrier((got_back, terms))
-    terms = pairwise(terms, (("y_lo", n_y), ("x", n_x)))
-    weight_grad = terms / math.sqrt(nodes * n_x * n_z * n_y)
-
-    sums = pl.pallas_call(
+    half = n_z // 2
+    low = feats * hidden // nodes
+    message = shape((feats + low, nodes), BF16)
+    plain = shape((feats, nodes), F32)
+    up, down, *sums = pl.pallas_call(
         gather_kernel,
-        out_shape=shape((n_z, feats, nodes), BF16),
+        out_shape=[message, message] + [plain] * (n_z - 2),
         in_specs=[SM, SM, VM],
-        out_specs=VM,
+        out_specs=[VM] * n_z,
         scratch_shapes=[pltpu.VMEM((n_z, blocks, feats, width), F32)],
-        compiler_params=params(12),
+        compiler_params=params(16),
         cost_estimate=cost(slots * feats * width, 4 * slots * feats * width),
         name="gather",
     )(me, want, got_back)
-    got_sums = swap(sums, "z")
-    embed_grad = pl.pallas_call(
-        combine_kernel,
-        out_shape=shape((feats, nodes), F32),
-        in_specs=[VM, VM],
-        out_specs=VM,
+    sums[half:half] = [None, None]
+    onward = [(i, (i + 1) % n_z) for i in range(n_z)]
+    back = [(i, (i - 1) % n_z) for i in range(n_z)]
+    places = [up] * n_z
+    for hop in range(half):
+        up = lax.ppermute(up, "z", onward)
+        places[n_z - 1 - hop] = up
+        if hop == half - 1:
+            break
+        down = lax.ppermute(down, "z", back)
+        places[hop + 1] = down
+        if hop < half - 2:
+            up, down = pl.pallas_call(
+                hop_kernel,
+                out_shape=(message, message),
+                in_specs=[VM] * 4,
+                out_specs=(VM, VM),
+                compiler_params=params(4),
+                name="hop",
+            )(up, down, sums[half - 1 - hop], sums[half + 2 + hop])
+        else:
+            up = pl.pallas_call(
+                hop_kernel,
+                out_shape=message,
+                in_specs=[VM] * 2,
+                out_specs=VM,
+                compiler_params=params(4),
+                name="hop",
+            )(up, sums[half - 1 - hop])
+    embed_grad, weight_grad = pl.pallas_call(
+        functools.partial(combine_kernel, 1.0 / math.sqrt(nodes * n_x * n_z * n_y)),
+        out_shape=(plain, shape((feats, hidden), F32)),
+        in_specs=[SM] + [VM] * (2 + n_z),
+        out_specs=(VM, VM),
+        scratch_shapes=[pltpu.VMEM((n_z, low, nodes), F32)],
         compiler_params=params(8),
-        cost_estimate=cost(n_z * feats * nodes, 2 * n_z * feats * nodes),
+        cost_estimate=cost(3 * feats * nodes, 16 * feats * nodes),
         name="combine",
-    )(got_sums, grad)
+    )(me, grad, sums[0], *places)
     return (out, embed_grad, weight_grad)
 
 

time: 167 us -> 156 us (0.934)
  waiting for transfers between devices: 71.4 us -> 30.7 us
  blocking collectives: 39.9 us -> 72.9 us
  local copies, waits for them, and re-layouts: 7.81 us -> 5.1 us
    ppermute x9 -> x3, waiting for transfers between devices: 41.4 us -> 8.31 us  [pairwise(): lax.ppermute(value, name, [(i, i ^ bit) for i in range(size)])]
    all_to_all x0 -> x1, blocking collectives: none -> 33 us  [per_device(): got_back = swap(send_back, plane)]
    all_to_all x2 -> x0, waiting for transfers between devices: 25.8 us -> none  [the longest x1 13 us: per_device(): got_sums = swap(sums, 'z')]
    ppermute x0 -> x7, waiting for transfers between devices: none -> 18.2 us  [the longest x4 11.6 us: per_device(): up = lax.ppermute(up, 'z', onward)]
    ppermute x0 -> x7, starting transfers between devices: none -> 8.99 us  [the longest x4 7.26 us: per_device(): up = lax.ppermute(up, 'z', onward)]
    all_to_all x2 -> x0, starting transfers between devices: 8.5 us -> none  [the longest x1 4.81 us: per_device(): got_back = swap(send_back, plane)]
    unnamed x26 -> x18, local copies, waits for them, and re-layouts: 5.62 us -> 2.93 us
    ppermute x9 -> x3, starting transfers between devices: 6.23 us -> 5.05 us  [pairwise(): lax.ppermute(value, name, [(i, i ^ bit) for i in range(size)])]
  transfers between devices with their start and end apart: 15 -> 14, of which waited for: 11 -> 9; matrix products, arithmetic and copies ran while one was open for 1% -> 1% of each run, Pallas kernels for 2% -> 3%
where the time goes in v3:
time: 156 us; the launch traced here: 155 us
  blocking collectives  72.9 us (47%)
  waiting for transfers between devices  30.7 us (20%)
  starting transfers between devices  26 us (17%)
  Pallas kernels  19.1 us (12%)
  local copies, waits for them, and re-layouts  5.1 us (3%)
    all_to_all x1, blocking collectives, per_device(): got_back = swap(send_back, plane)  33 us
    all_to_all x1, blocking collectives, per_device(): got = swap(send, plane)  31.9 us
    ppermute x4, waiting for transfers between devices, per_device(): up = lax.ppermute(up, 'z', onward)  11.6 us
    all_to_all x1, starting transfers between devices, per_device(): held = swap(jnp.broadcast_to(embed[None], (n_z, feats, nodes)), 'z')  8.47 us
    ppermute x3, waiting for transfers between devices, pairwise(): lax.ppermute(value, name, [(i, i ^ bit) for i in range(size)])  8.31 us
    all_gather x1, blocking collectives, per_device(): agg_full = lax.all_gather(agg, FEAT, axis=0, tiled=True)  8.02 us
    ppermute x4, starting transfers between devices, per_device(): up = lax.ppermute(up, 'z', onward)  7.26 us
    ppermute x3, waiting for transfers between devices, per_device(): down = lax.ppermute(down, 'z', back)  6.59 us
  transfers between devices with their start and end apart: 14, of which 9 were waited for; matrix products, arithmetic and copies ran while one was open for 1% of the time, Pallas kernels for 3%

profile of v3, /device:TPU:8, one launch (start us, length us, event | category | flops | bytes accessed | tf_op | source)
XLA Modules:
  0.0 155.4 jit_solution(5094865718242670289)
XLA Ops:
  0.7 2.1 %broadcast_in_dim.2 = bf16[8,64,1024]{2,1,0:T(8,128)(2,1)} broadcast(bf16[64,1024]{1,0:T(8,128)(2,1)} %own_ref.1), dimensions={1,2} | broadcast | bytes 1179648 | tf_op jit(solution)/shard_map/broadcast_in_dim | solution.py:262
  2.7 8.5 %all-to-all-start = ((bf16[8,64,1024]{2,1,0:T(8,128)(2,1)}), bf16[8,64,1024]{2,1,0:T(8,128)(2,1)}, u32[]{:S(2)}, u32[]{:S(2)}) async-start(bf16[8,64,1024]{2,1,0:T(8,128)(2,1)} %broadcast_in_dim.2), calls=%async_computation | async-start | bytes 2097152 | tf_op jit(solution)/shard_map/all_to_all | solution.py:262
  11.3 1.5 collective-permute-start.2
  12.8 1.2 collective-permute-start.1
  15.0 0.8 slots.1
  16.3 6.2 %collective-permute-done.3 = s32[8,128]{1,0:T(8,128)S(1)} collective-permute-done((s32[8,128]{1,0:T(8,128)S(1)}, s32[8,128]{1,0:T(8,128)S(1)}, u32[]{:S(2)}, u32[]{:S(2)}) %collective-permute-start.3) | collective-permute-done | bytes 4128 | tf_op jit(solution)/shard_map/ppermute | solution.py:245
  22.5 1.5 collective-permute-start.4
  24.0 2.1 %collective-permute-done.4 = s32[8,128]{1,0:T(8,128)S(1)} collective-permute-done((s32[8,128]{1,0:T(8,128)S(1)}, s32[8,128]{1,0:T(8,128)S(1)}, u32[]{:S(2)}, u32[]{:S(2)}) %collective-permute-start.4) | collective-permute-done | bytes 4128 | tf_op jit(solution)/shard_map/ppermute | solution.py:245
  26.1 3.0 %collective-permute-start.5 = (s32[8,128]{1,0:T(8,128)S(1)}, s32[8,128]{1,0:T(8,128)}, u32[]{:S(2)}, u32[]{:S(2)}) collective-permute-start(s32[8,128]{1,0:T(8,128)S(1)} %add.14), channel_id=1, source_target_pairs={{0,128},{64,192},{128,0},{192,64},{1,129},{65,193},{129,1},{193,65... | collective-permute-start | bytes 12296 | tf_op jit(solution)/shard_map/ppermute | solution.py:245
  29.2 2.8 %copy-done = s32[96,128,128]{2,1,0:T(8,128)S(1)} copy-done((s32[96,128,128]{2,1,0:T(8,128)S(1)}, s32[96,128,128]{2,1,0:T(8,128)}, u32[]{:S(2)}) %copy-start) | copy-done | bytes 6291480
  32.0 3.2 %masks.1 = (bf16[96,128,128]{2,1,0:T(8,128)(2,1)S(1)}, f32[8,8,128]{2,1,0:T(8,128)S(1)}) custom-call(s32[96]{0:T(128)S(1)} %copy-done.3, s32[96,128,128]{2,1,0:T(8,128)S(1)} %copy-done), custom_call_target="tpu_custom_call" | custom-call | flops 25165824 | bytes 9437184 | tf_op jit(solution)/shard_map/masks/pallas_call | solution.py:282
  35.9 4.2 %all-to-all-done.held_ref = bf16[8,64,1024]{2,1,0:T(8,128)(2,1)} async-done(((bf16[8,64,1024]{2,1,0:T(8,128)(2,1)}), bf16[8,64,1024]{2,1,0:T(8,128)(2,1)}, u32[]{:S(2)}, u32[]{:S(2)}) %all-to-all-start) | async-done | bytes 1048608 | tf_op jit(solution)/shard_map/all_to_all | solution.py:262
  40.0 1.8 %select.1 = bf16[128,64,128]{2,1,0:T(8,128)(2,1)S(1)} custom-call(s32[2]{0:T(128)S(1)} %pad_add_fusion.me_ref, s32[8,128]{1,0:T(8,128)S(1)} %add.15.want_ref, bf16[8,64,1024]{2,1,0:T(8,128)(2,1)} %all-to-all-done.held_ref), custom_call_target="tpu_custom_call" | custom-call | bytes 4194304 | tf_op jit(solution)/shard_map/select/pallas_call | solution.py:302
  41.9 31.9 %all_to_all.15.got_ref = bf16[128,64,128]{2,1,0:T(8,128)(2,1)S(1)} all-to-all(bf16[128,64,128]{2,1,0:T(8,128)(2,1)S(1)} %select.1), channel_id=1, replica_groups=mesh['x'=4,'z'=8,'y_lo'=2,'feat'=4] {'x','y_lo'}, dimensions={0} | all-to-all | bytes 4194304 | tf_op jit(solution)/shard_map/all_to_all | solution.py:311
  73.8 4.1 %forward.1.aggown_ref = bf16[64,1024]{1,0:T(8,128)(2,1)S(1)} custom-call(s32[96]{0:T(128)S(1)} %bitcast.7, s32[96]{0:T(128)S(1)} %copy-done.3, bf16[128,64,128]{2,1,0:T(8,128)(2,1)S(1)} %all_to_all.15.got_ref, bf16[96,128,128]{2,1,0:T(8,128)(2,1)S(1)} %get-tuple-element.39.mask_ref, bf16[64,1024]{1,0:T(8,128)(2,1)S(1)} %copy-done.1, ...), custom_call_target="tpu_custom_call" | custom-call | flops 201326592 | bytes 4718592 | tf_op jit(solution)/shard_map/forward/pallas_call | solution.py:313
  77.9 8.0 %all_gather.3.agg_ref = bf16[256,1024]{1,0:T(8,128)(2,1)S(1)} all-gather(bf16[64,1024]{1,0:T(8,128)(2,1)S(1)} %forward.1.aggown_ref), channel_id=1, replica_groups=mesh['x'=4,'z'=8,'y_lo'=2,'feat'=4] {'feat'}, dimensions={0}, use_global_device_ids=true | all-gather | bytes 655360 | tf_op jit(solution)/shard_map/all_gather | solution.py:324
  85.9 2.7 %dense.1 = (bf16[64,1024]{1,0:T(8,128)(2,1)}, f32[64,1024]{1,0:T(8,128)S(1)}, bf16[8,64,128]{2,1,0:T(8,128)(2,1)S(1)}, f32[64,256]{1,0:T(8,128)S(1)}) custom-call(s32[1]{0:T(128)} %bitcast.part_ref, bf16[256,1024]{1,0:T(8,128)(2,1)S(1)} %all_gather.3.agg_ref, bf16[64,1024]{1,0:T(8,128)(2,1)S(1)} %forward.1.aggown_ref, bf16[64,256]{1,0:T(8,128)(2,1)S(1)} %copy-done.2, ...), custom_call_target="tpu_custom_call" | custom-call | flops 201326592 | bytes 1572864 | tf_op jit(solution)/shard_map/dense/pallas_call | solution.py:325
  88.6 3.4 %backward.1 = bf16[8,1152,128]{2,1,0:T(8,128)(2,1)S(1)} custom-call(s32[96]{0:T(128)S(1)} %bitcast.8, s32[96]{0:T(128)S(1)} %copy-done.3, bf16[8,64,128]{2,1,0:T(8,128)(2,1)S(1)} %get-tuple-element.47.scaled_ref, bf16[96,128,128]{2,1,0:T(8,128)(2,1)S(1)} %get-tuple-element.39.mask_ref, f32[64,256]{1,0:T(8,128)S(1)} %get-tuple-element.48.terms_ref), custom_call_target="tpu_custom_call" | custom-call | flops 201326592 | bytes 4718592 | tf_op jit(solution)/shard_map/backward/pallas_call | solution.py:347
  92.0 33.0 %all_to_all.16.got_ref = bf16[8,1152,128]{2,1,0:T(8,128)(2,1)S(1)} all-to-all(bf16[8,1152,128]{2,1,0:T(8,128)(2,1)S(1)} %backward.1), channel_id=1, replica_groups=mesh['x'=4,'z'=8,'y_lo'=2,'feat'=4] {'x','y_lo'}, dimensions={0} | all-to-all | bytes 4718592 | tf_op jit(solution)/shard_map/all_to_all | solution.py:356
  125.0 1.7 %gather.1 = (bf16[80,1024]{1,0:T(8,128)(2,1)S(1)}, bf16[80,1024]{1,0:T(8,128)(2,1)S(1)}, f32[64,1024]{1,0:T(8,128)S(1)}, f32[64,1024]{1,0:T(8,128)S(1)}, f32[64,...) custom-call(s32[2]{0:T(128)S(1)} %pad_add_fusion.me_ref, ...), custom_call_target="tpu_custom_call" | custom-call | flops 1048576 | bytes 4194304 | tf_op jit(solution)/shard_map/gather/pallas_call | solution.py:362
  126.8 2.0 %collective-permute-start.7 = (bf16[80,1024]{1,0:T(8,128)(2,1)S(1)}, bf16[80,1024]{1,0:T(8,128)(2,1)S(1)}, u32[]{:S(2)}, u32[]{:S(2)}) collective-permute-start(bf16[80,1024]{1,0:T(8,128)(2,1)S(1)} %get-tuple-element.50.refs_0_), channel_id=1, source_target_pairs={{0,8},{8,16},{16,24},{24,32},{32,40},{40,48},{48,56},{56,0},{1,9},... | collective-permute-start | bytes 491528 | tf_op jit(solution)/shard_map/ppermute | solution.py:377
  128.8 3.3 %collective-permute-done.6.refs_1_ = bf16[80,1024]{1,0:T(8,128)(2,1)S(1)} collective-permute-done((bf16[80,1024]{1,0:T(8,128)(2,1)S(1)}, bf16[80,1024]{1,0:T(8,128)(2,1)S(1)}, u32[]{:S(2)}, u32[]{:S(2)}) %collective-permute-start.6) | collective-permute-done | bytes 163872 | tf_op jit(solution)/shard_map/ppermute | solution.py:381
  132.1 1.3 collective-permute-done.7.refs_0_.refs_7_
  133.6 2.0 %collective-permute-start.9 = (bf16[80,1024]{1,0:T(8,128)(2,1)S(1)}, bf16[80,1024]{1,0:T(8,128)(2,1)S(1)}, u32[]{:S(2)}, u32[]{:S(2)}) collective-permute-start(bf16[80,1024]{1,0:T(8,128)(2,1)S(1)} %get-tuple-element.55), channel_id=1, source_target_pairs={{0,8},{8,16},{16,24},{24,32},{32,40},{40,48},{48,56},{56,0},{1,9},... | collective-permute-start | bytes 491528 | tf_op jit(solution)/shard_map/ppermute | solution.py:377
  135.6 3.3 %collective-permute-done.8.refs_1_.refs_2_ = bf16[80,1024]{1,0:T(8,128)(2,1)S(1)} collective-permute-done((bf16[80,1024]{1,0:T(8,128)(2,1)S(1)}, bf16[80,1024]{1,0:T(8,128)(2,1)S(1)}, u32[]{:S(2)}, u32[]{:S(2)}) %collective-permute-start.8) | collective-permute-done | bytes 163872 | tf_op jit(solution)/shard_map/ppermute | solution.py:381
  138.9 1.3 collective-permute-done.9.refs_0_.refs_6_
  140.2 1.8 %collective-permute-start.11 = (bf16[80,1024]{1,0:T(8,128)(2,1)S(1)}, bf16[80,1024]{1,0:T(8,128)(2,1)S(1)}, u32[]{:S(2)}, u32[]{:S(2)}) collective-permute-start(bf16[80,1024]{1,0:T(8,128)(2,1)S(1)} %get-tuple-element.59), channel_id=1, source_target_pairs={{0,8},{8,16},{16,24},{24,32},{32,40},{40,48},{48,56},{56,0},{1,9},... | collective-permute-start | bytes 491528 | tf_op jit(solution)/shard_map/ppermute | solution.py:377
  142.0 1.6 %collective-permute-start.10 = (bf16[80,1024]{1,0:T(8,128)(2,1)S(1)}, bf16[80,1024]{1,0:T(8,128)(2,1)S(1)}, u32[]{:S(2)}, u32[]{:S(2)}) collective-permute-start(bf16[80,1024]{1,0:T(8,128)(2,1)S(1)} %get-tuple-element.58), channel_id=1, source_target_pairs={{0,56},{8,0},{16,8},{24,16},{32,24},{40,32},{48,40},{56,48},{1,57}... | collective-permute-start | bytes 491528 | tf_op jit(solution)/shard_map/ppermute | solution.py:381
  143.5 3.9 %collective-permute-done.11.refs_0_.refs_5_ = bf16[80,1024]{1,0:T(8,128)(2,1)S(1)} collective-permute-done((bf16[80,1024]{1,0:T(8,128)(2,1)S(1)}, bf16[80,1024]{1,0:T(8,128)(2,1)S(1)}, u32[]{:S(2)}, u32[]{:S(2)}) %collective-permute-start.11) | collective-permute-done | bytes 163872 | tf_op jit(solution)/shard_map/ppermute | solution.py:377
  147.4 1.5 collective-permute-start.12
  148.9 5.1 %collective-permute-done.12.refs_4_ = bf16[80,1024]{1,0:T(8,128)(2,1)S(1)} collective-permute-done((bf16[80,1024]{1,0:T(8,128)(2,1)S(1)}, bf16[80,1024]{1,0:T(8,128)(2,1)S(1)}, u32[]{:S(2)}, u32[]{:S(2)}) %collective-permute-start.12) | collective-permute-done | bytes 163872 | tf_op jit(solution)/shard_map/ppermute | solution.py:377
  154.1 1.3 combine.1
  (35 shorter events, 2.6 us)
Async XLA Ops:
  0.6 10.6 %copy-start.5 = (bf16[64,1024]{1,0:T(8,128)(2,1)S(1)}, bf16[64,1024]{1,0:T(8,128)(2,1)}, u32[]{:S(2)}) copy-start(bf16[64,1024]{1,0:T(8,128)(2,1)} %param.9) | copy-start | bytes 393220
  0.6 10.6 %copy-start.2 = (bf16[64,256]{1,0:T(8,128)(2,1)S(1)}, bf16[64,256]{1,0:T(8,128)(2,1)}, u32[]{:S(2)}) copy-start(bf16[64,256]{1,0:T(8,128)(2,1)} %weight_ref.1) | copy-start | bytes 98308
  0.7 14.1 %copy-start.7 = (s32[96]{0:T(128)S(1)}, s32[96]{0:T(128)}, u32[]{:S(2)}) copy-start(s32[96]{0:T(128)} %param.13) | copy-start | bytes 1156
  0.7 14.2 %copy-start.4 = (s32[96,1]{0,1:T(1,128)S(1)}, s32[96,1]{0,1:T(1,128)}, u32[]{:S(2)}) copy-start(s32[96,1]{0,1:T(1,128)} %param.12) | copy-start | bytes 1156
  0.7 28.5 %copy-start.3 = (s32[96]{0:T(128)S(1)}, s32[96]{0:T(128)}, u32[]{:S(2)}) copy-start(s32[96]{0:T(128)} %rows_ref.5) | copy-start | bytes 1156
  2.7 37.3 %all-to-all-start = ((bf16[8,64,1024]{2,1,0:T(8,128)(2,1)}), bf16[8,64,1024]{2,1,0:T(8,128)(2,1)}, u32[]{:S(2)}, u32[]{:S(2)}) async-start(bf16[8,64,1024]{2,1,0:T(8,128)(2,1)} %broadcast_in_dim.2), calls=%async_computation | async-start | bytes 2097152 | tf_op jit(solution)/shard_map/all_to_all | solution.py:262
  11.3 24.6 %collective-permute-start.2 = (bf16[64,1280]{1,0:T(8,128)(2,1)S(1)}, bf16[64,1280]{1,0:T(8,128)(2,1)S(1)}, u32[]{:S(2)}, u32[]{:S(2)}) collective-permute-start(bf16[64,1280]{1,0:T(8,128)(2,1)S(1)} %constant_dynamic-update-slice_fusion.refs_0_), channel_id=1, source_target_pairs={{0,3},{1,2},{2,1},{3,0},{4,7},{5,6},{6,5},{7,4},{8,11},{9,10},{10,... | collective-permute-start | bytes 491528 | tf_op jit(solution)/shard_map/ppermute | solution.py:279
  12.8 23.1 %collective-permute-start.1 = (bf16[64,1280]{1,0:T(8,128)(2,1)S(1)}, bf16[64,1280]{1,0:T(8,128)(2,1)}, u32[]{:S(2)}, u32[]{:S(2)}) collective-permute-start(bf16[64,1280]{1,0:T(8,128)(2,1)S(1)} %constant_dynamic-update-slice_fusion.refs_0_), channel_id=1, source_target_pairs={{0,2},{1,3},{2,0},{3,1},{4,6},{5,7},{6,4},{7,5},{8,10},{9,11},{10,... | collective-permute-start | bytes 491528 | tf_op jit(solution)/shard_map/ppermute | solution.py:279
  14.0 21.8 %collective-permute-start = (bf16[64,1280]{1,0:T(8,128)(2,1)S(1)}, bf16[64,1280]{1,0:T(8,128)(2,1)}, u32[]{:S(2)}, u32[]{:S(2)}) collective-permute-start(bf16[64,1280]{1,0:T(8,128)(2,1)S(1)} %constant_dynamic-update-slice_fusion.refs_0_), channel_id=1, source_target_pairs={{0,1},{1,0},{2,3},{3,2},{4,5},{5,4},{6,7},{7,6},{8,9},{9,8},{10,11... | collective-permute-start | bytes 491528 | tf_op jit(solution)/shard_map/ppermute | solution.py:279
  15.8 6.7 %collective-permute-start.3 = (s32[8,128]{1,0:T(8,128)S(1)}, s32[8,128]{1,0:T(8,128)S(1)}, u32[]{:S(2)}, u32[]{:S(2)}) collective-permute-start(s32[8,128]{1,0:T(8,128)S(1)} %get-tuple-element.37), channel_id=1, source_target_pairs={{0,4},{4,0},{1,5},{5,1},{2,6},{6,2},{3,7},{7,3},{8,12},{12,8},{9,1... | collective-permute-start | bytes 12296 | tf_op jit(solution)/shard_map/ppermute | solution.py:245
  22.5 3.6 %collective-permute-start.4 = (s32[8,128]{1,0:T(8,128)S(1)}, s32[8,128]{1,0:T(8,128)S(1)}, u32[]{:S(2)}, u32[]{:S(2)}) collective-permute-start(s32[8,128]{1,0:T(8,128)S(1)} %add.13), channel_id=1, source_target_pairs={{0,64},{64,0},{128,192},{192,128},{1,65},{65,1},{129,193},{193,129... | collective-permute-start | bytes 12296 | tf_op jit(solution)/shard_map/ppermute | solution.py:245
  26.1 9.0 %copy-start.6 = (s32[8,128]{1,0:T(8,128)}, s32[8,128]{1,0:T(8,128)S(1)}, u32[]{:S(2)}) copy-start(s32[8,128]{1,0:T(8,128)S(1)} %add.14) | copy-start | bytes 12292
  26.1 9.0 %collective-permute-start.5 = (s32[8,128]{1,0:T(8,128)S(1)}, s32[8,128]{1,0:T(8,128)}, u32[]{:S(2)}, u32[]{:S(2)}) collective-permute-start(s32[8,128]{1,0:T(8,128)S(1)} %add.14), channel_id=1, source_target_pairs={{0,128},{64,192},{128,0},{192,64},{1,129},{65,193},{129,1},{193,65... | collective-permute-start | bytes 12296 | tf_op jit(solution)/shard_map/ppermute | solution.py:245
  29.2 2.8 %copy-start = (s32[96,128,128]{2,1,0:T(8,128)S(1)}, s32[96,128,128]{2,1,0:T(8,128)}, u32[]{:S(2)}) copy-start(s32[96,128,128]{2,1,0:T(8,128)} %edge_ref.1) | copy-start | bytes 18874372
  41.9 31.9 %copy-start.1 = (bf16[64,1024]{1,0:T(8,128)(2,1)S(1)}, bf16[64,1024]{1,0:T(8,128)(2,1)}, u32[]{:S(2)}) copy-start(bf16[64,1024]{1,0:T(8,128)(2,1)} %own_ref.1) | copy-start | bytes 393220
  126.7 5.4 %collective-permute-start.6 = (bf16[80,1024]{1,0:T(8,128)(2,1)S(1)}, bf16[80,1024]{1,0:T(8,128)(2,1)S(1)}, u32[]{:S(2)}, u32[]{:S(2)}) collective-permute-start(bf16[80,1024]{1,0:T(8,128)(2,1)S(1)} %get-tuple-element.51), channel_id=1, source_target_pairs={{0,56},{8,0},{16,8},{24,16},{32,24},{40,32},{48,40},{56,48},{1,57}... | collective-permute-start | bytes 491528 | tf_op jit(solution)/shard_map/ppermute | solution.py:381
  126.8 6.6 %collective-permute-start.7 = (bf16[80,1024]{1,0:T(8,128)(2,1)S(1)}, bf16[80,1024]{1,0:T(8,128)(2,1)S(1)}, u32[]{:S(2)}, u32[]{:S(2)}) collective-permute-start(bf16[80,1024]{1,0:T(8,128)(2,1)S(1)} %get-tuple-element.50.refs_0_), channel_id=1, source_target_pairs={{0,8},{8,16},{16,24},{24,32},{32,40},{40,48},{48,56},{56,0},{1,9},... | collective-permute-start | bytes 491528 | tf_op jit(solution)/shard_map/ppermute | solution.py:377
  133.5 5.4 %collective-permute-start.8 = (bf16[80,1024]{1,0:T(8,128)(2,1)S(1)}, bf16[80,1024]{1,0:T(8,128)(2,1)S(1)}, u32[]{:S(2)}, u32[]{:S(2)}) collective-permute-start(bf16[80,1024]{1,0:T(8,128)(2,1)S(1)} %get-tuple-element.54), channel_id=1, source_target_pairs={{0,56},{8,0},{16,8},{24,16},{32,24},{40,32},{48,40},{56,48},{1,57}... | collective-permute-start | bytes 491528 | tf_op jit(solution)/shard_map/ppermute | solution.py:381
  133.6 6.6 %collective-permute-start.9 = (bf16[80,1024]{1,0:T(8,128)(2,1)S(1)}, bf16[80,1024]{1,0:T(8,128)(2,1)S(1)}, u32[]{:S(2)}, u32[]{:S(2)}) collective-permute-start(bf16[80,1024]{1,0:T(8,128)(2,1)S(1)} %get-tuple-element.55), channel_id=1, source_target_pairs={{0,8},{8,16},{16,24},{24,32},{32,40},{40,48},{48,56},{56,0},{1,9},... | collective-permute-start | bytes 491528 | tf_op jit(solution)/shard_map/ppermute | solution.py:377
  140.2 7.2 %collective-permute-start.11 = (bf16[80,1024]{1,0:T(8,128)(2,1)S(1)}, bf16[80,1024]{1,0:T(8,128)(2,1)S(1)}, u32[]{:S(2)}, u32[]{:S(2)}) collective-permute-start(bf16[80,1024]{1,0:T(8,128)(2,1)S(1)} %get-tuple-element.59), channel_id=1, source_target_pairs={{0,8},{8,16},{16,24},{24,32},{32,40},{40,48},{48,56},{56,0},{1,9},... | collective-permute-start | bytes 491528 | tf_op jit(solution)/shard_map/ppermute | solution.py:377
  142.0 7.0 %collective-permute-start.10 = (bf16[80,1024]{1,0:T(8,128)(2,1)S(1)}, bf16[80,1024]{1,0:T(8,128)(2,1)S(1)}, u32[]{:S(2)}, u32[]{:S(2)}) collective-permute-start(bf16[80,1024]{1,0:T(8,128)(2,1)S(1)} %get-tuple-element.58), channel_id=1, source_target_pairs={{0,56},{8,0},{16,8},{24,16},{32,24},{40,32},{48,40},{56,48},{1,57}... | collective-permute-start | bytes 491528 | tf_op jit(solution)/shard_map/ppermute | solution.py:381
  147.4 6.6 %collective-permute-start.12 = (bf16[80,1024]{1,0:T(8,128)(2,1)S(1)}, bf16[80,1024]{1,0:T(8,128)(2,1)S(1)}, u32[]{:S(2)}, u32[]{:S(2)}) collective-permute-start(bf16[80,1024]{1,0:T(8,128)(2,1)S(1)} %hop.5), channel_id=1, source_target_pairs={{0,8},{8,16},{16,24},{24,32},{32,40},{40,48},{48,56},{56,0},{1,9},... | collective-permute-start | bytes 491528 | tf_op jit(solution)/shard_map/ppermute | solution.py:377

commit v4 on v3

--- a/solution.py
+++ b/solution.py
@@ -60,70 +60,54 @@
     lax.fori_loop(0, readers, body, 0)
 
 
-def masks_kernel(rows_ref, edge_ref, mask_ref, root_ref, degree_ref):
-    step = pl.program_id(0)
-    many = edge_ref.shape[0]
-
-    @pl.when(step == 0)
-    def _():
-        degree_ref[...] = jnp.zeros_like(degree_ref)
-
-    ones = jnp.ones((8, edge_ref.shape[2]), BF16)
-    for j in range(many):
-        mask = edge_ref[j].astype(F32).astype(BF16)
-        mask_ref[j] = mask
-        count = lax.dot_general(ones, mask, (((1,), (1,)), ((), ())), preferred_element_type=F32)
-        row = rows_ref[step * many + j]
-        degree_ref[row] = degree_ref[row] + count
-
-    @pl.when(step == pl.num_programs(0) - 1)
-    def _():
-        root_ref[...] = 1.0 / jnp.sqrt(1.0 + degree_ref[...])
-
-
-def forward_kernel(slot_ref, rows_ref, got_ref, mask_ref, own_ref, root_ref, agg_ref, acc_ref):
-    tiles = mask_ref.shape[0]
-    blocks, _, width = acc_ref.shape
+def forward_kernel(slot_ref, rows_ref, got_ref, edge_ref, own_ref, agg_ref, root_ref, acc_ref):
+    tiles, width, _ = edge_ref.shape
+    blocks = acc_ref.shape[0]
+    feats = got_ref.shape[1]
     acc_ref[...] = jnp.zeros_like(acc_ref)
     group = 8
+    ones = jnp.ones((16, width), BF16)
 
     def body(step, carry):
         terms = []
         for j in range(group):
             tile = step * group + j
+            mask = edge_ref[tile].astype(F32).astype(BF16)
+            left = jnp.concatenate([got_ref[slot_ref[tile]], ones], axis=0)
             terms.append(
-                lax.dot_general(
-                    got_ref[slot_ref[tile]],
-                    mask_ref[tile],
-                    (((1,), (1,)), ((), ())),
-                    preferred_element_type=F32,
-                )
+                lax.dot_general(left, mask, (((1,), (1,)), ((), ())), preferred_element_type=F32)
             )
         for j in range(group):
             row = rows_ref[step * group + j]
-            acc_ref[row] = acc_ref[row] + terms[j]
+            acc_ref[row] = acc_ref[row] + terms[j][:feats + 8]
         return carry
 
     lax.fori_loop(0, tiles // group, body, 0)
     for r in range(blocks):
         cols = slice(r * width, (r + 1) * width)
+        root = 1.0 / jnp.sqrt(1.0 + acc_ref[r, feats:feats + 8, :])
+        root_ref[r] = root
         agg_ref[:, cols] = (
-            own_ref[:, cols].astype(F32) + acc_ref[r] * root_ref[r, 0:1, :]
+            own_ref[:, cols].astype(F32) + acc_ref[r, :feats, :] * root[0:1, :]
         ).astype(BF16)
 
 
+def order_kernel(part_ref, *refs):
+    full_ref = refs[-1]
+    for m, ref in enumerate(refs[:-1]):
+        feats = ref.shape[0]
+        start = pl.multiple_of((part_ref[0] ^ m) * feats, feats)
+        full_ref[pl.ds(start, feats), :] = ref[...]
+
+
 def dense_kernel(
-    part_ref, agg_ref, aggown_ref, weight_ref, root_ref, *refs
+    part_ref, agg_ref, aggown_ref, full_ref, weight_ref, root_ref,
+    out_ref, grad_ref, scaled_ref, terms_ref, act_ref,
 ):
-    out_ref, grad_ref, scaled_ref, terms_ref, act_ref, full_ref = refs[-6:]
-    parts = refs[:-6]
     nodes = agg_ref.shape[1]
     feats = weight_ref.shape[0]
     width = scaled_ref.shape[2]
     first = pl.multiple_of(part_ref[0] * feats, feats)
-    for m, ref in enumerate(parts):
-        start = pl.multiple_of((part_ref[0] ^ m) * feats, feats)
-        full_ref[pl.ds(start, feats), :] = ref[...]
     chunk = 2 * width
     terms = jnp.zeros(terms_ref.shape, F32)
     for c in range(nodes // chunk):
@@ -146,8 +130,8 @@
     terms_ref[...] = terms
 
 
-def backward_kernel(slot_ref, rows_ref, scaled_ref, mask_ref, terms_ref, send_ref):
-    tiles = mask_ref.shape[0]
+def backward_kernel(slot_ref, rows_ref, scaled_ref, edge_ref, terms_ref, send_ref):
+    tiles = edge_ref.shape[0]
     feats, hidden = terms_ref.shape
     width = send_ref.shape[2]
     end = send_ref.shape[1] - feats * hidden // width
@@ -161,7 +145,9 @@
             slot = slot_ref[tile]
             start = pl.multiple_of((slot % per_peer) * feats, feats)
             send_ref[slot // per_peer, pl.ds(start, feats), :] = jnp.dot(
-                scaled_ref[rows_ref[tile]], mask_ref[tile], preferred_element_type=F32
+                scaled_ref[rows_ref[tile]],
+                edge_ref[tile].astype(F32).astype(BF16),
+                preferred_element_type=F32,
             ).astype(BF16)
         return carry
 
@@ -172,38 +158,54 @@
             send_ref[p, end + h * feats:end + (h + 1) * feats, :] = part
 
 
-def gather_kernel(me_ref, want_ref, got_ref, up_ref, down_ref, *refs):
-    acc_ref = refs[-1]
-    sums = refs[:-1]
-    owners, blocks, feats, width = acc_ref.shape
+def add_up(distances, me_ref, want_ref, got_ref, acc_ref, owners):
+    _, blocks, feats, width = acc_ref.shape
     readers = want_ref.shape[0]
     base = me_ref[0] * (2 * owners)
-    acc_ref[...] = jnp.zeros_like(acc_ref)
 
     def body(reader, carry):
-        for z in range(owners):
+        for i, d in enumerate(distances):
+            z = (me_ref[1] + d) % owners
             for k in range(2):
                 block = want_ref[reader, base + 2 * z + k]
-                start = (2 * z + k) * feats
-                acc_ref[z, block] = acc_ref[z, block] + got_ref[reader, start:start + feats, :].astype(F32)
+                start = pl.multiple_of((2 * z + k) * feats, feats)
+                acc_ref[i, block] = acc_ref[i, block] + got_ref[reader, pl.ds(start, feats), :].astype(F32)
         return carry
 
     lax.fori_loop(0, readers, body, 0)
+
+
+def start_kernel(owners, me_ref, want_ref, got_ref, up_ref, down_ref, acc_ref):
+    _, blocks, feats, width = acc_ref.shape
+    half = owners // 2
+    acc_ref[...] = jnp.zeros_like(acc_ref)
+    add_up((half, half + 1), me_ref, want_ref, got_ref, acc_ref, owners)
     end = 2 * owners * feats
     low = up_ref.shape[0] - feats
     for h in range((got_ref.shape[1] - end) // low):
         rows = slice(end + h * low, end + (h + 1) * low)
         terms = got_ref[0, rows, :].astype(F32)
-        for q in range(1, readers):
+        for q in range(1, got_ref.shape[0]):
             terms = terms + got_ref[q, rows, :].astype(F32)
         up_ref[feats:, h * width:(h + 1) * width] = terms.astype(BF16)
         down_ref[feats:, h * width:(h + 1) * width] = terms.astype(BF16)
+    for i, ref in enumerate((up_ref, down_ref)):
+        for r in range(blocks):
+            ref[:feats, r * width:(r + 1) * width] = acc_ref[i, r].astype(BF16)
+
+
+def gather_kernel(owners, me_ref, want_ref, got_ref, grad_ref, *refs):
+    acc_ref = refs[-1]
+    _, blocks, feats, width = acc_ref.shape
     half = owners // 2
-    for d in range(owners):
-        ref = up_ref if d == half else down_ref if d == half + 1 else sums[d - 2 * (d > half)]
-        z = (me_ref[1] + d) % owners
+    acc_ref[...] = jnp.zeros_like(acc_ref)
+    for r in range(blocks):
+        acc_ref[0, r] = grad_ref[:, r * width:(r + 1) * width]
+    distances = [d for d in range(owners) if d not in (half, half + 1)]
+    add_up(distances, me_ref, want_ref, got_ref, acc_ref, owners)
+    for i, ref in enumerate(refs[:-1]):
         for r in range(blocks):
-            ref[:feats, r * width:(r + 1) * width] = acc_ref[z, r].astype(ref.dtype)
+            ref[:, r * width:(r + 1) * width] = acc_ref[i, r]
 
 
 def hop_kernel(*refs):
@@ -214,14 +216,14 @@
         on_ref[feats:, :] = got_ref[feats:, :]
 
 
-def combine_kernel(scale, me_ref, grad_ref, own_ref, *refs):
+def combine_kernel(scale, me_ref, own_ref, *refs):
     out_ref, weight_ref, terms_ref = refs[-3:]
     places = refs[:-3]
     planes = len(places)
     feats, hidden = weight_ref.shape
     low, nodes = terms_ref.shape[1:]
     half = planes // 2
-    out_ref[...] = grad_ref[...] + own_ref[...] + (
+    out_ref[...] = own_ref[...] + (
         places[planes - half][:feats, :].astype(F32) + places[half - 1][:feats, :].astype(F32)
     )
     for d, ref in enumerate(places):
@@ -271,34 +273,23 @@
         name="slots",
     )(me, tile_owner, tile_owner.reshape(1, tiles), tile_sub.reshape(tiles, 1))
     slot = slot.reshape(tiles)
-    want = pairwise(ask, (("y_lo", n_y), ("x", n_x)))
-
     mine = jnp.concatenate([cotangent, weight], axis=1)
     n_feat = hidden // feats
     parts = [mine] + [
         lax.ppermute(mine, FEAT, [(i, i ^ m) for i in range(n_feat)]) for m in range(1, n_feat)
     ]
-    many = math.gcd(tiles, 12)
-    mask, root = pl.pallas_call(
-        masks_kernel,
-        out_shape=(shape(edge_masks.shape, BF16), shape((blocks, 8, width), F32)),
-        grid_spec=pltpu.PrefetchScalarGridSpec(
-            num_scalar_prefetch=1,
-            grid=(tiles // many,),
-            in_specs=[pl.BlockSpec((many, width, width), lambda i, rows: (i, 0, 0))],
-            out_specs=[
-                pl.BlockSpec((many, width, width), lambda i, rows: (i, 0, 0)),
-                pl.BlockSpec((blocks, 8, width), lambda i, rows: (0, 0, 0)),
-            ],
-            scratch_shapes=[pltpu.VMEM((blocks, 8, width), F32)],
-        ),
-        compiler_params=params(8),
-        cost_estimate=cost(2 * tiles * 8 * width * width, 6 * tiles * width * width),
-        name="masks",
-    )(tile_rows, edge_masks)
+    want = pairwise(ask, (("y_lo", n_y), ("x", n_x)))
 
     part = lax.axis_index(FEAT).astype(jnp.int32).reshape(1)
-    held, parts, part, mask, root = lax.optimization_barrier((held, parts, part, mask, root))
+    full = pl.pallas_call(
+        order_kernel,
+        out_shape=shape((hidden, nodes + hidden), BF16),
+        in_specs=[SM] + [VM] * n_feat,
+        out_specs=VM,
+        compiler_params=params(4),
+        name="order",
+    )(part, *parts)
+    held, full, part = lax.optimization_barrier((held, full, part))
     send = pl.pallas_call(
         select_kernel,
         out_shape=shape((slots, feats, width), BF16),
@@ -310,16 +301,16 @@
     )(me, want, held)
     got = swap(send, plane)
 
-    agg = pl.pallas_call(
+    agg, root = pl.pallas_call(
         forward_kernel,
-        out_shape=shape((feats, nodes), BF16),
-        in_specs=[SM, SM, VM, VM, VM, VM],
-        out_specs=VM,
-        scratch_shapes=[pltpu.VMEM((blocks, feats, width), F32)],
-        compiler_params=params(12),
+        out_shape=(shape((feats, nodes), BF16), shape((blocks, 8, width), F32)),
+        in_specs=[SM, SM, VM, VM, VM],
+        out_specs=(VM, VM),
+        scratch_shapes=[pltpu.VMEM((blocks, feats + 8, width), F32)],
+        compiler_params=params(16),
         cost_estimate=cost(2 * tiles * feats * width * width, 2 * tiles * (feats + width) * width),
         name="forward",
-    )(slot, tile_rows, got, mask, embed, root)
+    )(slot, tile_rows, got, edge_masks, embed)
 
     agg_full = lax.all_gather(agg, FEAT, axis=0, tiled=True)
     out, grad, scaled, terms = pl.pallas_call(
@@ -330,18 +321,15 @@
             shape((blocks, feats, width), BF16),
             shape((feats, hidden), F32),
         ),
-        in_specs=[SM] + [VM] * (4 + n_feat),
+        in_specs=[SM] + [VM] * 5,
         out_specs=(VM, VM, VM, VM),
-        scratch_shapes=[
-            pltpu.VMEM((hidden, 2 * width), F32),
-            pltpu.VMEM((hidden, nodes + hidden), BF16),
-        ],
+        scratch_shapes=[pltpu.VMEM((hidden, 2 * width), F32)],
         compiler_params=params(16),
         cost_estimate=cost(
             2 * hidden * (hidden + 2 * feats) * nodes, 2 * hidden * nodes * 3, hidden * nodes
         ),
         name="dense",
-    )(part, agg_full, agg, weight, root, *parts)
+    )(part, agg_full, agg, full, weight, root)
 
     extra = feats * hidden // width
     send_back = pl.pallas_call(
@@ -352,24 +340,34 @@
         compiler_params=params(12),
         cost_estimate=cost(2 * tiles * feats * width * width, 2 * tiles * (feats + width) * width),
         name="backward",
-    )(slot, tile_rows, scaled, mask, terms)
+    )(slot, tile_rows, scaled, edge_masks, terms)
     got_back = swap(send_back, plane)
 
     half = n_z // 2
     low = feats * hidden // nodes
     message = shape((feats + low, nodes), BF16)
     plain = shape((feats, nodes), F32)
-    up, down, *sums = pl.pallas_call(
-        gather_kernel,
-        out_shape=[message, message] + [plain] * (n_z - 2),
+    up, down = pl.pallas_call(
+        functools.partial(start_kernel, n_z),
+        out_shape=(message, message),
         in_specs=[SM, SM, VM],
-        out_specs=[VM] * n_z,
-        scratch_shapes=[pltpu.VMEM((n_z, blocks, feats, width), F32)],
+        out_specs=(VM, VM),
+        scratch_shapes=[pltpu.VMEM((2, blocks, feats, width), F32)],
+        compiler_params=params(8),
+        cost_estimate=cost(slots * feats * width // 4, slots * feats * width),
+        name="start",
+    )(me, want, got_back)
+    sums = pl.pallas_call(
+        functools.partial(gather_kernel, n_z),
+        out_shape=[plain] * (n_z - 2),
+        in_specs=[SM, SM, VM, VM],
+        out_specs=[VM] * (n_z - 2),
+        scratch_shapes=[pltpu.VMEM((n_z - 2, blocks, feats, width), F32)],
         compiler_params=params(16),
         cost_estimate=cost(slots * feats * width, 4 * slots * feats * width),
         name="gather",
-    )(me, want, got_back)
-    sums[half:half] = [None, None]
+    )(me, want, got_back, grad)
+    sums = [*sums[:half], None, None, *sums[half:]]
     onward = [(i, (i + 1) % n_z) for i in range(n_z)]
     back = [(i, (i - 1) % n_z) for i in range(n_z)]
     places = [up] * n_z
@@ -401,13 +399,13 @@
     embed_grad, weight_grad = pl.pallas_call(
         functools.partial(combine_kernel, 1.0 / math.sqrt(nodes * n_x * n_z * n_y)),
         out_shape=(plain, shape((feats, hidden), F32)),
-        in_specs=[SM] + [VM] * (2 + n_z),
+        in_specs=[SM] + [VM] * (1 + n_z),
         out_specs=(VM, VM),
         scratch_shapes=[pltpu.VMEM((n_z, low, nodes), F32)],
         compiler_params=params(8),
         cost_estimate=cost(3 * feats * nodes, 16 * feats * nodes),
         name="combine",
-    )(me, grad, sums[0], *places)
+    )(me, sums[0], *places)
     return (out, embed_grad, weight_grad)
 
 

time: 156 us -> 153 us (0.981)
  waiting for transfers between devices: 30.7 us -> 35.6 us
  Pallas kernels: 19.1 us -> 15.4 us
  local copies, waits for them, and re-layouts: 5.1 us -> 2.35 us
    all_to_all x1, waiting for transfers between devices: 4.16 us -> 8.58 us  [per_device(): held = swap(jnp.broadcast_to(embed[None], (n_z, feats, nodes)), 'z')]
    unnamed x18 -> x16, local copies, waits for them, and re-layouts: 2.93 us -> 0.15 us
    ppermute x3, waiting for transfers between devices: 8.31 us -> 10.4 us  [pairwise(): lax.ppermute(value, name, [(i, i ^ bit) for i in range(size)])]
    pallas_call x3 -> x4, Pallas kernels: 8.99 us -> 6.94 us  [the longest x1 4.39 us: per_device(): pl.pallas_call(forward_kernel, out_shape=(shape((feats, nodes), BF16), sh...]
  transfers between devices with their start and end apart: 14 -> 14, of which waited for: 9 -> 10; matrix products, arithmetic and copies ran while one was open for 1% -> 0% of each run, Pallas kernels for 3% -> 2%
where the time goes in v4:
time: 153 us
  blocking collectives  72.9 us (48%)
  waiting for transfers between devices  35.6 us (23%)
  starting transfers between devices  26 us (17%)
  Pallas kernels  15.4 us (10%)
  local copies, waits for them, and re-layouts  2.35 us (2%)
    all_to_all x1, blocking collectives, per_device(): got_back = swap(send_back, plane)  33 us
    all_to_all x1, blocking collectives, per_device(): got = swap(send, plane)  31.9 us
    ppermute x4, waiting for transfers between devices, per_device(): up = lax.ppermute(up, 'z', onward)  11.6 us
    ppermute x3, waiting for transfers between devices, pairwise(): lax.ppermute(value, name, [(i, i ^ bit) for i in range(size)])  10.4 us
    all_to_all x1, waiting for transfers between devices, per_device(): held = swap(jnp.broadcast_to(embed[None], (n_z, feats, nodes)), 'z')  8.58 us
    all_to_all x1, starting transfers between devices, per_device(): held = swap(jnp.broadcast_to(embed[None], (n_z, feats, nodes)), 'z')  8.47 us
    all_gather x1, blocking collectives, per_device(): agg_full = lax.all_gather(agg, FEAT, axis=0, tiled=True)  8.02 us
    ppermute x4, starting transfers between devices, per_device(): up = lax.ppermute(up, 'z', onward)  7.25 us
  transfers between devices with their start and end apart: 14, of which 10 were waited for; matrix products, arithmetic and copies ran while one was open for 0% of the time, Pallas kernels for 2%

profile of v4, /device:TPU:8, one launch (start us, length us, event | category | flops | bytes accessed | tf_op | source)
XLA Modules:
  0.0 153.2 jit_solution(13953380540688854547)
XLA Ops:
  0.7 2.1 %broadcast_in_dim.2 = bf16[8,64,1024]{2,1,0:T(8,128)(2,1)} broadcast(bf16[64,1024]{1,0:T(8,128)(2,1)} %own_ref.1), dimensions={1,2} | broadcast | bytes 1179648 | tf_op jit(solution)/shard_map/broadcast_in_dim | solution.py:264
  2.8 8.5 %all-to-all-start = ((bf16[8,64,1024]{2,1,0:T(8,128)(2,1)}), bf16[8,64,1024]{2,1,0:T(8,128)(2,1)S(1)}, u32[]{:S(2)}, u32[]{:S(2)}) async-start(bf16[8,64,1024]{2,1,0:T(8,128)(2,1)} %broadcast_in_dim.2), calls=%async_computation | async-start | bytes 2097152 | tf_op jit(solution)/shard_map/all_to_all | solution.py:264
  11.3 1.5 %collective-permute-start.2 = (bf16[64,1280]{1,0:T(8,128)(2,1)S(1)}, bf16[64,1280]{1,0:T(8,128)(2,1)S(1)}, u32[]{:S(2)}, u32[]{:S(2)}) collective-permute-start(bf16[64,1280]{1,0:T(8,128)(2,1)S(1)} %constant_dynamic-update-slice_fusion.refs_0_), channel_id=1, source_target_pairs={{0,3},{1,2},{2,1},{3,0},{4,7},{5,6},{6,5},{7,4},{8,11},{9,10},{10,... | collective-permute-start | bytes 491528 | tf_op jit(solution)/shard_map/ppermute | solution.py:279
  12.8 1.2 collective-permute-start.1
  15.0 0.8 slots.1
  16.4 6.2 %collective-permute-done.3 = s32[8,128]{1,0:T(8,128)S(1)} collective-permute-done((s32[8,128]{1,0:T(8,128)S(1)}, s32[8,128]{1,0:T(8,128)S(1)}, u32[]{:S(2)}, u32[]{:S(2)}) %collective-permute-start.3) | collective-permute-done | bytes 4128 | tf_op jit(solution)/shard_map/ppermute | solution.py:247
  22.5 1.5 collective-permute-start.4
  24.1 2.1 %collective-permute-done.4 = s32[8,128]{1,0:T(8,128)S(1)} collective-permute-done((s32[8,128]{1,0:T(8,128)S(1)}, s32[8,128]{1,0:T(8,128)S(1)}, u32[]{:S(2)}, u32[]{:S(2)}) %collective-permute-start.4) | collective-permute-done | bytes 4128 | tf_op jit(solution)/shard_map/ppermute | solution.py:247
  26.2 3.0 %collective-permute-start.5 = (s32[8,128]{1,0:T(8,128)S(1)}, s32[8,128]{1,0:T(8,128)S(1)}, u32[]{:S(2)}, u32[]{:S(2)}) collective-permute-start(s32[8,128]{1,0:T(8,128)S(1)} %add.14), channel_id=1, source_target_pairs={{0,128},{64,192},{128,0},{192,64},{1,129},{65,193},{129,1},{193,65... | collective-permute-start | bytes 12296 | tf_op jit(solution)/shard_map/ppermute | solution.py:247
  29.2 2.1 %collective-permute-done.5 = s32[8,128]{1,0:T(8,128)S(1)} collective-permute-done((s32[8,128]{1,0:T(8,128)S(1)}, s32[8,128]{1,0:T(8,128)S(1)}, u32[]{:S(2)}, u32[]{:S(2)}) %collective-permute-start.5) | collective-permute-done | bytes 4128 | tf_op jit(solution)/shard_map/ppermute | solution.py:247
  31.4 8.6 %all-to-all-done.held_ref = bf16[8,64,1024]{2,1,0:T(8,128)(2,1)S(1)} async-done(((bf16[8,64,1024]{2,1,0:T(8,128)(2,1)}), bf16[8,64,1024]{2,1,0:T(8,128)(2,1)S(1)}, u32[]{:S(2)}, u32[]{:S(2)}) %all-to-all-start) | async-done | bytes 1048608 | tf_op jit(solution)/shard_map/all_to_all | solution.py:264
  40.0 1.2 select.1
  41.2 31.9 %all_to_all.15.got_ref = bf16[128,64,128]{2,1,0:T(8,128)(2,1)S(1)} all-to-all(bf16[128,64,128]{2,1,0:T(8,128)(2,1)S(1)} %select.1), channel_id=1, replica_groups=mesh['x'=4,'z'=8,'y_lo'=2,'feat'=4] {'x','y_lo'}, dimensions={0} | all-to-all | bytes 4194304 | tf_op jit(solution)/shard_map/all_to_all | solution.py:302
  73.1 4.4 %forward.1 = (bf16[64,1024]{1,0:T(8,128)(2,1)S(1)}, f32[8,8,128]{2,1,0:T(8,128)S(1)}) custom-call(s32[96]{0:T(128)S(1)} %bitcast.7, s32[96]{0:T(128)S(1)} %copy-done.4, bf16[128,64,128]{2,1,0:T(8,128)(2,1)S(1)} %all_to_all.15.got_ref, s32[96,128,128]{2,1,0:T(8,128)S(1)} %copy-done, bf16[64,1024]{1,0:T(8,128)(2,1)S(1)} %copy-done.1), custom_call_target="tpu_custom_call" | custom-call | flops 201326592 | bytes 4718592 | tf_op jit(solution)/shard_map/forward/pallas_call | solution.py:304
  77.5 8.0 %all_gather.3.agg_ref = bf16[256,1024]{1,0:T(8,128)(2,1)S(1)} all-gather(bf16[64,1024]{1,0:T(8,128)(2,1)S(1)} %get-tuple-element.32.aggown_ref), channel_id=1, replica_groups=mesh['x'=4,'z'=8,'y_lo'=2,'feat'=4] {'feat'}, dimensions={0}, use_global_device_ids=true | all-gather | bytes 655360 | tf_op jit(solution)/shard_map/all_gather | solution.py:315
  85.5 1.7 %dense.1 = (bf16[64,1024]{1,0:T(8,128)(2,1)}, f32[64,1024]{1,0:T(8,128)S(1)}, bf16[8,64,128]{2,1,0:T(8,128)(2,1)S(1)}, f32[64,256]{1,0:T(8,128)S(1)}) custom-call(s32[1]{0:T(128)} %bitcast.part_ref, bf16[256,1024]{1,0:T(8,128)(2,1)S(1)} %all_gather.3.agg_ref, bf16[64,1024]{1,0:T(8,128)(2,1)S(1)} %get-tuple-element.32.aggown_ref, ...), custom_call_target="tpu_custom_call" | custom-call | flops 201326592 | bytes 1572864 | tf_op jit(solution)/shard_map/dense/pallas_call | solution.py:316
  87.2 3.4 %backward.1 = bf16[8,1152,128]{2,1,0:T(8,128)(2,1)S(1)} custom-call(s32[96]{0:T(128)S(1)} %bitcast.8, s32[96]{0:T(128)S(1)} %copy-done.4, bf16[8,64,128]{2,1,0:T(8,128)(2,1)S(1)} %get-tuple-element.36.scaled_ref, s32[96,128,128]{2,1,0:T(8,128)S(1)} %copy-done, f32[64,256]{1,0:T(8,128)S(1)} %get-tuple-element.37.terms_ref), custom_call_target="tpu_custom_call" | custom-call | flops 201326592 | bytes 4718592 | tf_op jit(solution)/shard_map/backward/pallas_call | solution.py:335
  90.6 33.0 %all_to_all.16.got_ref = bf16[8,1152,128]{2,1,0:T(8,128)(2,1)S(1)} all-to-all(bf16[8,1152,128]{2,1,0:T(8,128)(2,1)S(1)} %backward.1), channel_id=1, replica_groups=mesh['x'=4,'z'=8,'y_lo'=2,'feat'=4] {'x','y_lo'}, dimensions={0} | all-to-all | bytes 4718592 | tf_op jit(solution)/shard_map/all_to_all | solution.py:344
  123.6 1.0 start.1
  124.7 2.0 %collective-permute-start.7 = (bf16[80,1024]{1,0:T(8,128)(2,1)S(1)}, bf16[80,1024]{1,0:T(8,128)(2,1)S(1)}, u32[]{:S(2)}, u32[]{:S(2)}) collective-permute-start(bf16[80,1024]{1,0:T(8,128)(2,1)S(1)} %get-tuple-element.40.refs_0_), channel_id=1, source_target_pairs={{0,8},{8,16},{16,24},{24,32},{32,40},{40,48},{48,56},{56,0},{1,9},... | collective-permute-start | bytes 491528 | tf_op jit(solution)/shard_map/ppermute | solution.py:375
  126.7 1.5 gather.1
  128.2 1.8 %collective-permute-done.6.refs_1_ = bf16[80,1024]{1,0:T(8,128)(2,1)S(1)} collective-permute-done((bf16[80,1024]{1,0:T(8,128)(2,1)S(1)}, bf16[80,1024]{1,0:T(8,128)(2,1)S(1)}, u32[]{:S(2)}, u32[]{:S(2)}) %collective-permute-start.6) | collective-permute-done | bytes 163872 | tf_op jit(solution)/shard_map/ppermute | solution.py:379
  130.0 1.3 collective-permute-done.7.refs_0_.refs_7_
  131.4 2.0 %collective-permute-start.9 = (bf16[80,1024]{1,0:T(8,128)(2,1)S(1)}, bf16[80,1024]{1,0:T(8,128)(2,1)S(1)}, u32[]{:S(2)}, u32[]{:S(2)}) collective-permute-start(bf16[80,1024]{1,0:T(8,128)(2,1)S(1)} %get-tuple-element.45), channel_id=1, source_target_pairs={{0,8},{8,16},{16,24},{24,32},{32,40},{40,48},{48,56},{56,0},{1,9},... | collective-permute-start | bytes 491528 | tf_op jit(solution)/shard_map/ppermute | solution.py:375
  133.4 3.3 %collective-permute-done.8.refs_1_.refs_2_ = bf16[80,1024]{1,0:T(8,128)(2,1)S(1)} collective-permute-done((bf16[80,1024]{1,0:T(8,128)(2,1)S(1)}, bf16[80,1024]{1,0:T(8,128)(2,1)S(1)}, u32[]{:S(2)}, u32[]{:S(2)}) %collective-permute-start.8) | collective-permute-done | bytes 163872 | tf_op jit(solution)/shard_map/ppermute | solution.py:379
  136.7 1.3 collective-permute-done.9.refs_0_.refs_6_
  138.1 1.7 %collective-permute-start.11 = (bf16[80,1024]{1,0:T(8,128)(2,1)S(1)}, bf16[80,1024]{1,0:T(8,128)(2,1)S(1)}, u32[]{:S(2)}, u32[]{:S(2)}) collective-permute-start(bf16[80,1024]{1,0:T(8,128)(2,1)S(1)} %get-tuple-element.49), channel_id=1, source_target_pairs={{0,8},{8,16},{16,24},{24,32},{32,40},{40,48},{48,56},{56,0},{1,9},... | collective-permute-start | bytes 491528 | tf_op jit(solution)/shard_map/ppermute | solution.py:375
  139.8 1.6 %collective-permute-start.10 = (bf16[80,1024]{1,0:T(8,128)(2,1)S(1)}, bf16[80,1024]{1,0:T(8,128)(2,1)S(1)}, u32[]{:S(2)}, u32[]{:S(2)}) collective-permute-start(bf16[80,1024]{1,0:T(8,128)(2,1)S(1)} %get-tuple-element.48), channel_id=1, source_target_pairs={{0,56},{8,0},{16,8},{24,16},{32,24},{40,32},{48,40},{56,48},{1,57}... | collective-permute-start | bytes 491528 | tf_op jit(solution)/shard_map/ppermute | solution.py:379
  141.4 3.9 %collective-permute-done.11.refs_0_.refs_5_ = bf16[80,1024]{1,0:T(8,128)(2,1)S(1)} collective-permute-done((bf16[80,1024]{1,0:T(8,128)(2,1)S(1)}, bf16[80,1024]{1,0:T(8,128)(2,1)S(1)}, u32[]{:S(2)}, u32[]{:S(2)}) %collective-permute-start.11) | collective-permute-done | bytes 163872 | tf_op jit(solution)/shard_map/ppermute | solution.py:375
  145.3 1.5 collective-permute-start.12
  146.8 5.1 %collective-permute-done.12.refs_4_ = bf16[80,1024]{1,0:T(8,128)(2,1)S(1)} collective-permute-done((bf16[80,1024]{1,0:T(8,128)(2,1)S(1)}, bf16[80,1024]{1,0:T(8,128)(2,1)S(1)}, u32[]{:S(2)}, u32[]{:S(2)}) %collective-permute-start.12) | collective-permute-done | bytes 163872 | tf_op jit(solution)/shard_map/ppermute | solution.py:375
  151.9 1.3 combine.1
  (34 shorter events, 1.9 us)
Async XLA Ops:
  0.6 10.6 %copy-start.5 = (bf16[64,1024]{1,0:T(8,128)(2,1)S(1)}, bf16[64,1024]{1,0:T(8,128)(2,1)}, u32[]{:S(2)}) copy-start(bf16[64,1024]{1,0:T(8,128)(2,1)} %param.9) | copy-start | bytes 393220
  0.6 10.6 %copy-start.2 = (bf16[64,256]{1,0:T(8,128)(2,1)S(1)}, bf16[64,256]{1,0:T(8,128)(2,1)}, u32[]{:S(2)}) copy-start(bf16[64,256]{1,0:T(8,128)(2,1)} %weight_ref.1) | copy-start | bytes 98308
  0.7 14.1 %copy-start.6 = (s32[96]{0:T(128)S(1)}, s32[96]{0:T(128)}, u32[]{:S(2)}) copy-start(s32[96]{0:T(128)} %param.13) | copy-start | bytes 1156
  0.7 14.2 %copy-start.3 = (s32[96,1]{0,1:T(1,128)S(1)}, s32[96,1]{0,1:T(1,128)}, u32[]{:S(2)}) copy-start(s32[96,1]{0,1:T(1,128)} %param.12) | copy-start | bytes 1156
  2.8 37.2 %all-to-all-start = ((bf16[8,64,1024]{2,1,0:T(8,128)(2,1)}), bf16[8,64,1024]{2,1,0:T(8,128)(2,1)S(1)}, u32[]{:S(2)}, u32[]{:S(2)}) async-start(bf16[8,64,1024]{2,1,0:T(8,128)(2,1)} %broadcast_in_dim.2), calls=%async_computation | async-start | bytes 2097152 | tf_op jit(solution)/shard_map/all_to_all | solution.py:264
  11.3 20.0 %collective-permute-start.2 = (bf16[64,1280]{1,0:T(8,128)(2,1)S(1)}, bf16[64,1280]{1,0:T(8,128)(2,1)S(1)}, u32[]{:S(2)}, u32[]{:S(2)}) collective-permute-start(bf16[64,1280]{1,0:T(8,128)(2,1)S(1)} %constant_dynamic-update-slice_fusion.refs_0_), channel_id=1, source_target_pairs={{0,3},{1,2},{2,1},{3,0},{4,7},{5,6},{6,5},{7,4},{8,11},{9,10},{10,... | collective-permute-start | bytes 491528 | tf_op jit(solution)/shard_map/ppermute | solution.py:279
  12.8 18.5 %collective-permute-start.1 = (bf16[64,1280]{1,0:T(8,128)(2,1)S(1)}, bf16[64,1280]{1,0:T(8,128)(2,1)S(1)}, u32[]{:S(2)}, u32[]{:S(2)}) collective-permute-start(bf16[64,1280]{1,0:T(8,128)(2,1)S(1)} %constant_dynamic-update-slice_fusion.refs_0_), channel_id=1, source_target_pairs={{0,2},{1,3},{2,0},{3,1},{4,6},{5,7},{6,4},{7,5},{8,10},{9,11},{10,... | collective-permute-start | bytes 491528 | tf_op jit(solution)/shard_map/ppermute | solution.py:279
  14.1 17.3 %collective-permute-start = (bf16[64,1280]{1,0:T(8,128)(2,1)S(1)}, bf16[64,1280]{1,0:T(8,128)(2,1)S(1)}, u32[]{:S(2)}, u32[]{:S(2)}) collective-permute-start(bf16[64,1280]{1,0:T(8,128)(2,1)S(1)} %constant_dynamic-update-slice_fusion.refs_0_), channel_id=1, source_target_pairs={{0,1},{1,0},{2,3},{3,2},{4,5},{5,4},{6,7},{7,6},{8,9},{9,8},{10,11... | collective-permute-start | bytes 491528 | tf_op jit(solution)/shard_map/ppermute | solution.py:279
  15.8 6.7 %collective-permute-start.3 = (s32[8,128]{1,0:T(8,128)S(1)}, s32[8,128]{1,0:T(8,128)S(1)}, u32[]{:S(2)}, u32[]{:S(2)}) collective-permute-start(s32[8,128]{1,0:T(8,128)S(1)} %get-tuple-element.30), channel_id=1, source_target_pairs={{0,4},{4,0},{1,5},{5,1},{2,6},{6,2},{3,7},{7,3},{8,12},{12,8},{9,1... | collective-permute-start | bytes 12296 | tf_op jit(solution)/shard_map/ppermute | solution.py:247
  22.5 3.6 %collective-permute-start.4 = (s32[8,128]{1,0:T(8,128)S(1)}, s32[8,128]{1,0:T(8,128)S(1)}, u32[]{:S(2)}, u32[]{:S(2)}) collective-permute-start(s32[8,128]{1,0:T(8,128)S(1)} %add.13), channel_id=1, source_target_pairs={{0,64},{64,0},{128,192},{192,128},{1,65},{65,1},{129,193},{193,129... | collective-permute-start | bytes 12296 | tf_op jit(solution)/shard_map/ppermute | solution.py:247
  26.2 5.1 %collective-permute-start.5 = (s32[8,128]{1,0:T(8,128)S(1)}, s32[8,128]{1,0:T(8,128)S(1)}, u32[]{:S(2)}, u32[]{:S(2)}) collective-permute-start(s32[8,128]{1,0:T(8,128)S(1)} %add.14), channel_id=1, source_target_pairs={{0,128},{64,192},{128,0},{192,64},{1,129},{65,193},{129,1},{193,65... | collective-permute-start | bytes 12296 | tf_op jit(solution)/shard_map/ppermute | solution.py:247
  40.0 33.1 %copy-start = (s32[96,128,128]{2,1,0:T(8,128)S(1)}, s32[96,128,128]{2,1,0:T(8,128)}, u32[]{:S(2)}) copy-start(s32[96,128,128]{2,1,0:T(8,128)} %edge_ref.3) | copy-start | bytes 18874372
  41.2 31.9 %copy-start.1 = (bf16[64,1024]{1,0:T(8,128)(2,1)S(1)}, bf16[64,1024]{1,0:T(8,128)(2,1)}, u32[]{:S(2)}) copy-start(bf16[64,1024]{1,0:T(8,128)(2,1)} %own_ref.1) | copy-start | bytes 393220
  41.2 31.9 %copy-start.4 = (s32[96]{0:T(128)S(1)}, s32[96]{0:T(128)}, u32[]{:S(2)}) copy-start(s32[96]{0:T(128)} %rows_ref.3) | copy-start | bytes 1156
  124.6 5.4 %collective-permute-start.6 = (bf16[80,1024]{1,0:T(8,128)(2,1)S(1)}, bf16[80,1024]{1,0:T(8,128)(2,1)S(1)}, u32[]{:S(2)}, u32[]{:S(2)}) collective-permute-start(bf16[80,1024]{1,0:T(8,128)(2,1)S(1)} %get-tuple-element.41), channel_id=1, source_target_pairs={{0,56},{8,0},{16,8},{24,16},{32,24},{40,32},{48,40},{56,48},{1,57}... | collective-permute-start | bytes 491528 | tf_op jit(solution)/shard_map/ppermute | solution.py:379
  124.7 6.6 %collective-permute-start.7 = (bf16[80,1024]{1,0:T(8,128)(2,1)S(1)}, bf16[80,1024]{1,0:T(8,128)(2,1)S(1)}, u32[]{:S(2)}, u32[]{:S(2)}) collective-permute-start(bf16[80,1024]{1,0:T(8,128)(2,1)S(1)} %get-tuple-element.40.refs_0_), channel_id=1, source_target_pairs={{0,8},{8,16},{16,24},{24,32},{32,40},{40,48},{48,56},{56,0},{1,9},... | collective-permute-start | bytes 491528 | tf_op jit(solution)/shard_map/ppermute | solution.py:375
  131.3 5.4 %collective-permute-start.8 = (bf16[80,1024]{1,0:T(8,128)(2,1)S(1)}, bf16[80,1024]{1,0:T(8,128)(2,1)S(1)}, u32[]{:S(2)}, u32[]{:S(2)}) collective-permute-start(bf16[80,1024]{1,0:T(8,128)(2,1)S(1)} %get-tuple-element.44), channel_id=1, source_target_pairs={{0,56},{8,0},{16,8},{24,16},{32,24},{40,32},{48,40},{56,48},{1,57}... | collective-permute-start | bytes 491528 | tf_op jit(solution)/shard_map/ppermute | solution.py:379
  131.4 6.6 %collective-permute-start.9 = (bf16[80,1024]{1,0:T(8,128)(2,1)S(1)}, bf16[80,1024]{1,0:T(8,128)(2,1)S(1)}, u32[]{:S(2)}, u32[]{:S(2)}) collective-permute-start(bf16[80,1024]{1,0:T(8,128)(2,1)S(1)} %get-tuple-element.45), channel_id=1, source_target_pairs={{0,8},{8,16},{16,24},{24,32},{32,40},{40,48},{48,56},{56,0},{1,9},... | collective-permute-start | bytes 491528 | tf_op jit(solution)/shard_map/ppermute | solution.py:375
  138.1 7.2 %collective-permute-start.11 = (bf16[80,1024]{1,0:T(8,128)(2,1)S(1)}, bf16[80,1024]{1,0:T(8,128)(2,1)S(1)}, u32[]{:S(2)}, u32[]{:S(2)}) collective-permute-start(bf16[80,1024]{1,0:T(8,128)(2,1)S(1)} %get-tuple-element.49), channel_id=1, source_target_pairs={{0,8},{8,16},{16,24},{24,32},{32,40},{40,48},{48,56},{56,0},{1,9},... | collective-permute-start | bytes 491528 | tf_op jit(solution)/shard_map/ppermute | solution.py:375
  139.8 7.0 %collective-permute-start.10 = (bf16[80,1024]{1,0:T(8,128)(2,1)S(1)}, bf16[80,1024]{1,0:T(8,128)(2,1)S(1)}, u32[]{:S(2)}, u32[]{:S(2)}) collective-permute-start(bf16[80,1024]{1,0:T(8,128)(2,1)S(1)} %get-tuple-element.48), channel_id=1, source_target_pairs={{0,56},{8,0},{16,8},{24,16},{32,24},{40,32},{48,40},{56,48},{1,57}... | collective-permute-start | bytes 491528 | tf_op jit(solution)/shard_map/ppermute | solution.py:379
  145.3 6.6 %collective-permute-start.12 = (bf16[80,1024]{1,0:T(8,128)(2,1)S(1)}, bf16[80,1024]{1,0:T(8,128)(2,1)S(1)}, u32[]{:S(2)}, u32[]{:S(2)}) collective-permute-start(bf16[80,1024]{1,0:T(8,128)(2,1)S(1)} %hop.5), channel_id=1, source_target_pairs={{0,8},{8,16},{16,24},{24,32},{32,40},{40,48},{48,56},{56,0},{1,9},... | collective-permute-start | bytes 491528 | tf_op jit(solution)/shard_map/ppermute | solution.py:375

commit v5 on v4

--- a/solution.py
+++ b/solution.py
@@ -44,17 +44,20 @@
     ask_ref[...] = jnp.where(row == me_ref[0], jnp.sum(asked, axis=0, keepdims=True), 0)
 
 
-def select_kernel(me_ref, want_ref, held_ref, send_ref):
+def select_kernel(me_ref, want_ref, *refs):
+    send_ref = refs[-1]
+    held = refs[:-1]
     readers = want_ref.shape[0]
-    owners = held_ref.shape[0]
+    owners = len(held)
     width = send_ref.shape[2]
     base = me_ref[0] * (2 * owners)
 
     def body(reader, carry):
-        for z in range(owners):
+        for d, ref in enumerate(held):
+            z = (me_ref[1] + d) % owners
             for k in range(2):
                 start = pl.multiple_of(want_ref[reader, base + 2 * z + k] * width, width)
-                send_ref[(reader * owners + z) * 2 + k] = held_ref[z, :, pl.ds(start, width)]
+                send_ref[(reader * owners + z) * 2 + k] = ref[:, pl.ds(start, width)]
         return carry
 
     lax.fori_loop(0, readers, body, 0)
@@ -261,7 +264,6 @@
     shape = jax.ShapeDtypeStruct
     swap = functools.partial(lax.all_to_all, split_axis=0, concat_axis=0, tiled=True)
 
-    held = swap(jnp.broadcast_to(embed[None], (n_z, feats, nodes)), "z")
     me = jnp.stack([lax.axis_index("x") * n_y + lax.axis_index("y_lo"), lax.axis_index("z")])
     me = me.astype(jnp.int32)
     ask, slot = pl.pallas_call(
@@ -278,7 +280,28 @@
     parts = [mine] + [
         lax.ppermute(mine, FEAT, [(i, i ^ m) for i in range(n_feat)]) for m in range(1, n_feat)
     ]
-    want = pairwise(ask, (("y_lo", n_y), ("x", n_x)))
+    onward = [(i, (i + 1) % n_z) for i in range(n_z)]
+    back = [(i, (i - 1) % n_z) for i in range(n_z)]
+    half = n_z // 2
+    held = [embed] * n_z
+    up = down = embed
+    steps = [("y_lo", n_y, 1), ("x", n_x, 1), ("x", n_x, 2)]
+    for hop in range(half):
+        up = lax.ppermute(up, "z", onward)
+        if hop < half - 1:
+            down = lax.ppermute(down, "z", back)
+        if hop < len(steps):
+            name, size, bit = steps[hop]
+            ask = ask + lax.ppermute(ask, name, [(i, i ^ bit) for i in range(size)])
+        if hop < half - 1:
+            if hop == 1:
+                up, down, ask, *parts = lax.optimization_barrier((up, down, ask, *parts))
+            else:
+                up, down, ask = lax.optimization_barrier((up, down, ask))
+        held[n_z - 1 - hop] = up
+        if hop < half - 1:
+            held[hop + 1] = down
+    want = ask
 
     part = lax.axis_index(FEAT).astype(jnp.int32).reshape(1)
     full = pl.pallas_call(
@@ -293,12 +316,12 @@
     send = pl.pallas_call(
         select_kernel,
         out_shape=shape((slots, feats, width), BF16),
-        in_specs=[SM, SM, VM],
+        in_specs=[SM, SM] + [VM] * n_z,
         out_specs=VM,
         compiler_params=params(8),
         cost_estimate=cost(0, 2 * slots * feats * width * 2),
         name="select",
-    )(me, want, held)
+    )(me, want, *held)
     got = swap(send, plane)
 
     agg, root = pl.pallas_call(
@@ -343,7 +366,6 @@
     )(slot, tile_rows, scaled, edge_masks, terms)
     got_back = swap(send_back, plane)
 
-    half = n_z // 2
     low = feats * hidden // nodes
     message = shape((feats + low, nodes), BF16)
     plain = shape((feats, nodes), F32)
@@ -368,8 +390,6 @@
         name="gather",
     )(me, want, got_back, grad)
     sums = [*sums[:half], None, None, *sums[half:]]
-    onward = [(i, (i + 1) % n_z) for i in range(n_z)]
-    back = [(i, (i - 1) % n_z) for i in range(n_z)]
     places = [up] * n_z
     for hop in range(half):
         up = lax.ppermute(up, "z", onward)

time: 153 us -> 152 us (level)
  blocking collectives: 72.9 us -> 69.6 us
  waiting for transfers between devices: 35.6 us -> 32.7 us
  local copies, waits for them, and re-layouts: 2.35 us -> 4.76 us
  starting transfers between devices: 26 us -> 28.2 us
    ppermute x4 -> x8, waiting for transfers between devices: 11.6 us -> 22.5 us  [per_device(): up = lax.ppermute(up, 'z', onward)]
    ppermute x3 -> x6, starting transfers between devices: 1.76 us -> 12.4 us  [per_device(): down = lax.ppermute(down, 'z', back)]
    all_to_all x1 -> x0, waiting for transfers between devices: 8.58 us -> none  [per_device(): held = swap(jnp.broadcast_to(embed[None], (n_z, feats, nodes)), 'z')]
    all_to_all x1 -> x0, starting transfers between devices: 8.47 us -> none  [per_device(): held = swap(jnp.broadcast_to(embed[None], (n_z, feats, nodes)), 'z')]
    ppermute x3, waiting for transfers between devices: 10.4 us -> 2.39 us  [per_device(): ask = ask + lax.ppermute(ask, name, [(i, i ^ bit) for i in range(size)])]
    all_to_all x1, blocking collectives: 31.9 us -> 28.8 us  [per_device(): got = swap(send, plane)]
    unnamed x16 -> x14, local copies, waits for them, and re-layouts: 0.15 us -> 3.25 us
    ppermute x3, waiting for transfers between devices: 0.01 us -> 2.67 us  [per_device(): lax.ppermute(mine, FEAT, [(i, i ^ m) for i in range(n_feat)])]
  transfers between devices with their start and end apart: 14 -> 20, of which waited for: 10 -> 10; matrix products, arithmetic and copies ran while one was open for 0% -> 2% of each run, Pallas kernels for 2% -> 2%
where the time goes in v5:
time: 152 us
  blocking collectives  69.6 us (46%)
  waiting for transfers between devices  32.7 us (22%)
  starting transfers between devices  28.2 us (19%)
  Pallas kernels  16 us (11%)
  local copies, waits for them, and re-layouts  4.76 us (3%)
    all_to_all x1, blocking collectives, per_device(): got_back = swap(send_back, plane)  32.8 us
    all_to_all x1, blocking collectives, per_device(): got = swap(send, plane)  28.8 us
    ppermute x8, waiting for transfers between devices, per_device(): up = lax.ppermute(up, 'z', onward)  22.5 us
    ppermute x6, starting transfers between devices, per_device(): down = lax.ppermute(down, 'z', back)  12.4 us
    all_gather x1, blocking collectives, per_device(): agg_full = lax.all_gather(agg, FEAT, axis=0, tiled=True)  8.02 us
    ppermute x8, starting transfers between devices, per_device(): up = lax.ppermute(up, 'z', onward)  7.65 us
    ppermute x6, waiting for transfers between devices, per_device(): down = lax.ppermute(down, 'z', back)  5.1 us
    ppermute x3, starting transfers between devices, per_device(): ask = ask + lax.ppermute(ask, name, [(i, i ^ bit) for i in range(size)])  4.84 us
  transfers between devices with their start and end apart: 20, of which 10 were waited for; matrix products, arithmetic and copies ran while one was open for 2% of the time, Pallas kernels for 2%

profile of v5, /device:TPU:8, one launch (start us, length us, event | category | flops | bytes accessed | tf_op | source)
XLA Modules:
  0.0 152.1 jit_solution(8075368563554449902)
XLA Ops:
  0.6 5.9 %collective-permute-start.1 = (bf16[64,1024]{1,0:T(8,128)(2,1)}, bf16[64,1024]{1,0:T(8,128)(2,1)S(1)}, u32[]{:S(2)}, u32[]{:S(2)}) collective-permute-start(bf16[64,1024]{1,0:T(8,128)(2,1)} %own_ref.1), channel_id=1, source_target_pairs={{0,56},{8,0},{16,8},{24,16},{32,24},{40,32},{48,40},{56,48},{1,57}... | collective-permute-start | bytes 393224 | tf_op jit(solution)/shard_map/ppermute | solution.py:292
  11.8 1.5 collective-permute-start.8
  13.3 1.2 collective-permute-start.7
  15.2 1.6 %collective-permute-start.5 = (s32[8,128]{1,0:T(8,128)S(1)}, s32[8,128]{1,0:T(8,128)S(1)}, u32[]{:S(2)}, u32[]{:S(2)}) collective-permute-start(s32[8,128]{1,0:T(8,128)S(1)} %add.13), channel_id=1, source_target_pairs={{0,64},{64,0},{128,192},{192,128},{1,65},{65,1},{129,193},{193,129... | collective-permute-start | bytes 12296 | tf_op jit(solution)/shard_map/ppermute | solution.py:295
  16.8 3.2 %collective-permute-start.4 = (bf16[64,1024]{1,0:T(8,128)(2,1)S(1)}, bf16[64,1024]{1,0:T(8,128)(2,1)S(1)}, u32[]{:S(2)}, u32[]{:S(2)}) collective-permute-start(bf16[64,1024]{1,0:T(8,128)(2,1)S(1)} %collective-permute-done.1.refs_1_), channel_id=1, source_target_pairs={{0,56},{8,0},{16,8},{24,16},{32,24},{40,32},{48,40},{56,48},{1,57}... | collective-permute-start | bytes 393224 | tf_op jit(solution)/shard_map/ppermute | solution.py:292
  20.0 2.7 %collective-permute-done.7.refs_2_ = bf16[64,1280]{1,0:T(8,128)(2,1)S(1)} collective-permute-done((bf16[64,1280]{1,0:T(8,128)(2,1)S(1)}, bf16[64,1280]{1,0:T(8,128)(2,1)S(1)}, u32[]{:S(2)}, u32[]{:S(2)}) %collective-permute-start.7) | collective-permute-done | bytes 163872 | tf_op jit(solution)/shard_map/ppermute | solution.py:281
  22.7 3.5 %collective-permute-done.3.refs_6_ = bf16[64,1024]{1,0:T(8,128)(2,1)S(1)} collective-permute-done((bf16[64,1024]{1,0:T(8,128)(2,1)S(1)}, bf16[64,1024]{1,0:T(8,128)(2,1)S(1)}, u32[]{:S(2)}, u32[]{:S(2)}) %collective-permute-start.3) | collective-permute-done | bytes 131104 | tf_op jit(solution)/shard_map/ppermute | solution.py:290
  27.1 1.1 collective-permute-start.9
  28.2 2.7 %collective-permute-start.11 = (s32[8,128]{1,0:T(8,128)S(1)}, s32[8,128]{1,0:T(8,128)S(1)}, u32[]{:S(2)}, u32[]{:S(2)}) collective-permute-start(s32[8,128]{1,0:T(8,128)S(1)} %add.14), channel_id=1, source_target_pairs={{0,128},{64,192},{128,0},{192,64},{1,129},{65,193},{129,1},{193,65... | collective-permute-start | bytes 12296 | tf_op jit(solution)/shard_map/ppermute | solution.py:295
  31.0 2.4 %collective-permute-done.11 = s32[8,128]{1,0:T(8,128)S(1)} collective-permute-done((s32[8,128]{1,0:T(8,128)S(1)}, s32[8,128]{1,0:T(8,128)S(1)}, u32[]{:S(2)}, u32[]{:S(2)}) %collective-permute-start.11) | collective-permute-done | bytes 4128 | tf_op jit(solution)/shard_map/ppermute | solution.py:295
  33.5 6.1 %collective-permute-done.12.refs_4_ = bf16[64,1024]{1,0:T(8,128)(2,1)S(1)} collective-permute-done((bf16[64,1024]{1,0:T(8,128)(2,1)S(1)}, bf16[64,1024]{1,0:T(8,128)(2,1)S(1)}, u32[]{:S(2)}, u32[]{:S(2)}) %collective-permute-start.12) | collective-permute-done | bytes 131104 | tf_op jit(solution)/shard_map/ppermute | solution.py:290
  40.5 1.8 %select.1 = bf16[128,64,128]{2,1,0:T(8,128)(2,1)S(1)} custom-call(s32[2]{0:T(128)S(1)} %pad_add_fusion.me_ref, s32[8,128]{1,0:T(8,128)S(1)} %add.15.want_ref, bf16[64,1024]{1,0:T(8,128)(2,1)S(1)} %copy-done.1, bf16[64,1024]{1,0:T(8,128)(2,1)S(1)} %collective-permute-done.1.refs_1_, bf16[64,1024]{1,0:T(8,128)(2,1)S(1)} %collective-permute-done.4.refs_2_, ...), custom_call_target="tpu_custom_call" | custom-call | bytes 4194304 | tf_op jit(solution)/shard_map/select/pallas_call | solution.py:316
  42.4 28.8 %all_to_all.10.got_ref = bf16[128,64,128]{2,1,0:T(8,128)(2,1)S(1)} all-to-all(bf16[128,64,128]{2,1,0:T(8,128)(2,1)S(1)} %select.1), channel_id=1, replica_groups=mesh['x'=4,'z'=8,'y_lo'=2,'feat'=4] {'x','y_lo'}, dimensions={0} | all-to-all | bytes 4194304 | tf_op jit(solution)/shard_map/all_to_all | solution.py:325
  71.1 4.4 %forward.1 = (bf16[64,1024]{1,0:T(8,128)(2,1)S(1)}, f32[8,8,128]{2,1,0:T(8,128)S(1)}) custom-call(s32[96]{0:T(128)S(1)} %bitcast.7, s32[96]{0:T(128)S(1)} %copy-done.5, bf16[128,64,128]{2,1,0:T(8,128)(2,1)S(1)} %all_to_all.10.got_ref, s32[96,128,128]{2,1,0:T(8,128)S(1)} %copy-done, bf16[64,1024]{1,0:T(8,128)(2,1)S(1)} %copy-done.2), custom_call_target="tpu_custom_call" | custom-call | flops 201326592 | bytes 4718592 | tf_op jit(solution)/shard_map/forward/pallas_call | solution.py:327
  75.5 8.0 %all_gather.3.agg_ref = bf16[256,1024]{1,0:T(8,128)(2,1)S(1)} all-gather(bf16[64,1024]{1,0:T(8,128)(2,1)S(1)} %get-tuple-element.72.aggown_ref), channel_id=1, replica_groups=mesh['x'=4,'z'=8,'y_lo'=2,'feat'=4] {'feat'}, dimensions={0}, use_global_device_ids=true | all-gather | bytes 655360 | tf_op jit(solution)/shard_map/all_gather | solution.py:338
  83.6 1.7 %dense.1 = (bf16[64,1024]{1,0:T(8,128)(2,1)}, f32[64,1024]{1,0:T(8,128)S(1)}, bf16[8,64,128]{2,1,0:T(8,128)(2,1)S(1)}, f32[64,256]{1,0:T(8,128)S(1)}) custom-call(s32[1]{0:T(128)} %bitcast.4.part_ref, bf16[256,1024]{1,0:T(8,128)(2,1)S(1)} %all_gather.3.agg_ref, bf16[64,1024]{1,0:T(8,128)(2,1)S(1)} %get-tuple-element.72.aggown_ref, ...), custom_call_target="tpu_custom_call" | custom-call | flops 201326592 | bytes 1572864 | tf_op jit(solution)/shard_map/dense/pallas_call | solution.py:339
  85.2 3.4 %backward.1 = bf16[8,1152,128]{2,1,0:T(8,128)(2,1)S(1)} custom-call(s32[96]{0:T(128)S(1)} %bitcast.8, s32[96]{0:T(128)S(1)} %copy-done.5, bf16[8,64,128]{2,1,0:T(8,128)(2,1)S(1)} %get-tuple-element.76.scaled_ref, s32[96,128,128]{2,1,0:T(8,128)S(1)} %copy-done, f32[64,256]{1,0:T(8,128)S(1)} %get-tuple-element.77.terms_ref), custom_call_target="tpu_custom_call" | custom-call | flops 201326592 | bytes 4718592 | tf_op jit(solution)/shard_map/backward/pallas_call | solution.py:358
  88.6 32.8 %all_to_all.11.got_ref = bf16[8,1152,128]{2,1,0:T(8,128)(2,1)S(1)} all-to-all(bf16[8,1152,128]{2,1,0:T(8,128)(2,1)S(1)} %backward.1), channel_id=1, replica_groups=mesh['x'=4,'z'=8,'y_lo'=2,'feat'=4] {'x','y_lo'}, dimensions={0} | all-to-all | bytes 4718592 | tf_op jit(solution)/shard_map/all_to_all | solution.py:367
  121.4 1.0 start.1
  123.3 1.3 collective-permute-start.14
  124.7 1.5 gather.1
  126.2 1.8 %collective-permute-done.13.refs_1_ = bf16[80,1024]{1,0:T(8,128)(2,1)S(1)} collective-permute-done((bf16[80,1024]{1,0:T(8,128)(2,1)S(1)}, bf16[80,1024]{1,0:T(8,128)(2,1)S(1)}, u32[]{:S(2)}, u32[]{:S(2)}) %collective-permute-start.13) | collective-permute-done | bytes 163872 | tf_op jit(solution)/shard_map/ppermute | solution.py:399
  128.0 1.9 %collective-permute-done.14.refs_0_.refs_7_ = bf16[80,1024]{1,0:T(8,128)(2,1)S(1)} collective-permute-done((bf16[80,1024]{1,0:T(8,128)(2,1)S(1)}, bf16[80,1024]{1,0:T(8,128)(2,1)S(1)}, u32[]{:S(2)}, u32[]{:S(2)}) %collective-permute-start.14) | collective-permute-done | bytes 163872 | tf_op jit(solution)/shard_map/ppermute | solution.py:395
  130.0 2.0 %collective-permute-start.16 = (bf16[80,1024]{1,0:T(8,128)(2,1)S(1)}, bf16[80,1024]{1,0:T(8,128)(2,1)S(1)}, u32[]{:S(2)}, u32[]{:S(2)}) collective-permute-start(bf16[80,1024]{1,0:T(8,128)(2,1)S(1)} %get-tuple-element.85), channel_id=1, source_target_pairs={{0,8},{8,16},{16,24},{24,32},{32,40},{40,48},{48,56},{56,0},{1,9},... | collective-permute-start | bytes 491528 | tf_op jit(solution)/shard_map/ppermute | solution.py:395
  132.0 3.3 %collective-permute-done.15.refs_1_.refs_2_ = bf16[80,1024]{1,0:T(8,128)(2,1)S(1)} collective-permute-done((bf16[80,1024]{1,0:T(8,128)(2,1)S(1)}, bf16[80,1024]{1,0:T(8,128)(2,1)S(1)}, u32[]{:S(2)}, u32[]{:S(2)}) %collective-permute-start.15) | collective-permute-done | bytes 163872 | tf_op jit(solution)/shard_map/ppermute | solution.py:399
  135.3 1.3 collective-permute-done.16.refs_0_.refs_6_
  136.7 2.0 %collective-permute-start.18 = (bf16[80,1024]{1,0:T(8,128)(2,1)S(1)}, bf16[80,1024]{1,0:T(8,128)(2,1)S(1)}, u32[]{:S(2)}, u32[]{:S(2)}) collective-permute-start(bf16[80,1024]{1,0:T(8,128)(2,1)S(1)} %get-tuple-element.89), channel_id=1, source_target_pairs={{0,8},{8,16},{16,24},{24,32},{32,40},{40,48},{48,56},{56,0},{1,9},... | collective-permute-start | bytes 491528 | tf_op jit(solution)/shard_map/ppermute | solution.py:395
  138.7 1.3 collective-permute-start.17
  140.0 4.2 %collective-permute-done.18.refs_0_.refs_5_ = bf16[80,1024]{1,0:T(8,128)(2,1)S(1)} collective-permute-done((bf16[80,1024]{1,0:T(8,128)(2,1)S(1)}, bf16[80,1024]{1,0:T(8,128)(2,1)S(1)}, u32[]{:S(2)}, u32[]{:S(2)}) %collective-permute-start.18) | collective-permute-done | bytes 163872 | tf_op jit(solution)/shard_map/ppermute | solution.py:395
  144.2 1.0 collective-permute-start.19
  145.3 5.6 %collective-permute-done.19.refs_4_ = bf16[80,1024]{1,0:T(8,128)(2,1)S(1)} collective-permute-done((bf16[80,1024]{1,0:T(8,128)(2,1)S(1)}, bf16[80,1024]{1,0:T(8,128)(2,1)S(1)}, u32[]{:S(2)}, u32[]{:S(2)}) %collective-permute-start.19) | collective-permute-done | bytes 163872 | tf_op jit(solution)/shard_map/ppermute | solution.py:395
  150.8 1.3 combine.1
  (43 shorter events, 9.2 us)
Async XLA Ops:
  0.6 14.6 %collective-permute-start.1 = (bf16[64,1024]{1,0:T(8,128)(2,1)}, bf16[64,1024]{1,0:T(8,128)(2,1)S(1)}, u32[]{:S(2)}, u32[]{:S(2)}) collective-permute-start(bf16[64,1024]{1,0:T(8,128)(2,1)} %own_ref.1), channel_id=1, source_target_pairs={{0,56},{8,0},{16,8},{24,16},{32,24},{40,32},{48,40},{56,48},{1,57}... | collective-permute-start | bytes 393224 | tf_op jit(solution)/shard_map/ppermute | solution.py:292
  6.6 8.6 %collective-permute-start = (bf16[64,1024]{1,0:T(8,128)(2,1)}, bf16[64,1024]{1,0:T(8,128)(2,1)S(1)}, u32[]{:S(2)}, u32[]{:S(2)}) collective-permute-start(bf16[64,1024]{1,0:T(8,128)(2,1)} %own_ref.1), channel_id=1, source_target_pairs={{0,8},{8,16},{16,24},{24,32},{32,40},{40,48},{48,56},{56,0},{1,9},... | collective-permute-start | bytes 393224 | tf_op jit(solution)/shard_map/ppermute | solution.py:290
  8.2 0.7 copy-start.4
  9.6 4.8 %collective-permute-start.2 = (s32[8,128]{1,0:T(8,128)S(1)}, s32[8,128]{1,0:T(8,128)S(1)}, u32[]{:S(2)}, u32[]{:S(2)}) collective-permute-start(s32[8,128]{1,0:T(8,128)S(1)} %get-tuple-element.48), channel_id=1, source_target_pairs={{0,4},{4,0},{1,5},{5,1},{2,6},{6,2},{3,7},{7,3},{8,12},{12,8},{9,1... | collective-permute-start | bytes 12296 | tf_op jit(solution)/shard_map/ppermute | solution.py:295
  11.8 8.2 %collective-permute-start.8 = (bf16[64,1280]{1,0:T(8,128)(2,1)S(1)}, bf16[64,1280]{1,0:T(8,128)(2,1)S(1)}, u32[]{:S(2)}, u32[]{:S(2)}) collective-permute-start(bf16[64,1280]{1,0:T(8,128)(2,1)S(1)} %constant_dynamic-update-slice_fusion.refs_0_), channel_id=1, source_target_pairs={{0,3},{1,2},{2,1},{3,0},{4,7},{5,6},{6,5},{7,4},{8,11},{9,10},{10,... | collective-permute-start | bytes 491528 | tf_op jit(solution)/shard_map/ppermute | solution.py:281
  13.3 9.4 %collective-permute-start.7 = (bf16[64,1280]{1,0:T(8,128)(2,1)S(1)}, bf16[64,1280]{1,0:T(8,128)(2,1)S(1)}, u32[]{:S(2)}, u32[]{:S(2)}) collective-permute-start(bf16[64,1280]{1,0:T(8,128)(2,1)S(1)} %constant_dynamic-update-slice_fusion.refs_0_), channel_id=1, source_target_pairs={{0,2},{1,3},{2,0},{3,1},{4,6},{5,7},{6,4},{7,5},{8,10},{9,11},{10,... | collective-permute-start | bytes 491528 | tf_op jit(solution)/shard_map/ppermute | solution.py:281
  14.4 8.3 %collective-permute-start.6 = (bf16[64,1280]{1,0:T(8,128)(2,1)S(1)}, bf16[64,1280]{1,0:T(8,128)(2,1)S(1)}, u32[]{:S(2)}, u32[]{:S(2)}) collective-permute-start(bf16[64,1280]{1,0:T(8,128)(2,1)S(1)} %constant_dynamic-update-slice_fusion.refs_0_), channel_id=1, source_target_pairs={{0,1},{1,0},{2,3},{3,2},{4,5},{5,4},{6,7},{7,6},{8,9},{9,8},{10,11... | collective-permute-start | bytes 491528 | tf_op jit(solution)/shard_map/ppermute | solution.py:281
  15.2 4.8 %collective-permute-start.5 = (s32[8,128]{1,0:T(8,128)S(1)}, s32[8,128]{1,0:T(8,128)S(1)}, u32[]{:S(2)}, u32[]{:S(2)}) collective-permute-start(s32[8,128]{1,0:T(8,128)S(1)} %add.13), channel_id=1, source_target_pairs={{0,64},{64,0},{128,192},{192,128},{1,65},{65,1},{129,193},{193,129... | collective-permute-start | bytes 12296 | tf_op jit(solution)/shard_map/ppermute | solution.py:295
  16.8 5.9 %collective-permute-start.4 = (bf16[64,1024]{1,0:T(8,128)(2,1)S(1)}, bf16[64,1024]{1,0:T(8,128)(2,1)S(1)}, u32[]{:S(2)}, u32[]{:S(2)}) collective-permute-start(bf16[64,1024]{1,0:T(8,128)(2,1)S(1)} %collective-permute-done.1.refs_1_), channel_id=1, source_target_pairs={{0,56},{8,0},{16,8},{24,16},{32,24},{40,32},{48,40},{56,48},{1,57}... | collective-permute-start | bytes 393224 | tf_op jit(solution)/shard_map/ppermute | solution.py:292
  20.0 6.2 %collective-permute-start.3 = (bf16[64,1024]{1,0:T(8,128)(2,1)S(1)}, bf16[64,1024]{1,0:T(8,128)(2,1)S(1)}, u32[]{:S(2)}, u32[]{:S(2)}) collective-permute-start(bf16[64,1024]{1,0:T(8,128)(2,1)S(1)} %collective-permute-done.refs_7_), channel_id=1, source_target_pairs={{0,8},{8,16},{16,24},{24,32},{32,40},{40,48},{48,56},{56,0},{1,9},... | collective-permute-start | bytes 393224 | tf_op jit(solution)/shard_map/ppermute | solution.py:290
  26.2 7.1 %collective-permute-start.10 = (bf16[64,1024]{1,0:T(8,128)(2,1)S(1)}, bf16[64,1024]{1,0:T(8,128)(2,1)S(1)}, u32[]{:S(2)}, u32[]{:S(2)}) collective-permute-start(bf16[64,1024]{1,0:T(8,128)(2,1)S(1)} %collective-permute-done.4.refs_2_), channel_id=1, source_target_pairs={{0,56},{8,0},{16,8},{24,16},{32,24},{40,32},{48,40},{56,48},{1,57}... | collective-permute-start | bytes 393224 | tf_op jit(solution)/shard_map/ppermute | solution.py:292
  27.1 6.2 %collective-permute-start.9 = (bf16[64,1024]{1,0:T(8,128)(2,1)S(1)}, bf16[64,1024]{1,0:T(8,128)(2,1)S(1)}, u32[]{:S(2)}, u32[]{:S(2)}) collective-permute-start(bf16[64,1024]{1,0:T(8,128)(2,1)S(1)} %collective-permute-done.3.refs_6_), channel_id=1, source_target_pairs={{0,8},{8,16},{16,24},{24,32},{32,40},{40,48},{48,56},{56,0},{1,9},... | collective-permute-start | bytes 393224 | tf_op jit(solution)/shard_map/ppermute | solution.py:290
  28.2 5.1 %collective-permute-start.11 = (s32[8,128]{1,0:T(8,128)S(1)}, s32[8,128]{1,0:T(8,128)S(1)}, u32[]{:S(2)}, u32[]{:S(2)}) collective-permute-start(s32[8,128]{1,0:T(8,128)S(1)} %add.14), channel_id=1, source_target_pairs={{0,128},{64,192},{128,0},{192,64},{1,129},{65,193},{129,1},{193,65... | collective-permute-start | bytes 12296 | tf_op jit(solution)/shard_map/ppermute | solution.py:295
  33.3 6.3 %collective-permute-start.12 = (bf16[64,1024]{1,0:T(8,128)(2,1)S(1)}, bf16[64,1024]{1,0:T(8,128)(2,1)S(1)}, u32[]{:S(2)}, u32[]{:S(2)}) collective-permute-start(bf16[64,1024]{1,0:T(8,128)(2,1)S(1)} %collective-permute-done.9.refs_5_), channel_id=1, source_target_pairs={{0,8},{8,16},{16,24},{24,32},{32,40},{40,48},{48,56},{56,0},{1,9},... | collective-permute-start | bytes 393224 | tf_op jit(solution)/shard_map/ppermute | solution.py:290
  39.6 0.9 copy-start.1
  40.5 30.6 %copy-start = (s32[96,128,128]{2,1,0:T(8,128)S(1)}, s32[96,128,128]{2,1,0:T(8,128)}, u32[]{:S(2)}) copy-start(s32[96,128,128]{2,1,0:T(8,128)} %edge_ref.3) | copy-start | bytes 18874372
  42.3 28.8 %copy-start.2 = (bf16[64,1024]{1,0:T(8,128)(2,1)S(1)}, bf16[64,1024]{1,0:T(8,128)(2,1)}, u32[]{:S(2)}) copy-start(bf16[64,1024]{1,0:T(8,128)(2,1)} %own_ref.1) | copy-start | bytes 393220
  42.4 28.8 %copy-start.5 = (s32[96]{0:T(128)S(1)}, s32[96]{0:T(128)}, u32[]{:S(2)}) copy-start(s32[96]{0:T(128)} %rows_ref.3) | copy-start | bytes 1156
  71.1 12.4 %copy-start.3 = (bf16[64,256]{1,0:T(8,128)(2,1)S(1)}, bf16[64,256]{1,0:T(8,128)(2,1)}, u32[]{:S(2)}) copy-start(bf16[64,256]{1,0:T(8,128)(2,1)} %weight_ref.1) | copy-start | bytes 98308
  122.4 5.6 %collective-permute-start.13 = (bf16[80,1024]{1,0:T(8,128)(2,1)S(1)}, bf16[80,1024]{1,0:T(8,128)(2,1)S(1)}, u32[]{:S(2)}, u32[]{:S(2)}) collective-permute-start(bf16[80,1024]{1,0:T(8,128)(2,1)S(1)} %get-tuple-element.81), channel_id=1, source_target_pairs={{0,56},{8,0},{16,8},{24,16},{32,24},{40,32},{48,40},{56,48},{1,57}... | collective-permute-start | bytes 491528 | tf_op jit(solution)/shard_map/ppermute | solution.py:399
  123.3 6.5 %collective-permute-start.14 = (bf16[80,1024]{1,0:T(8,128)(2,1)S(1)}, bf16[80,1024]{1,0:T(8,128)(2,1)S(1)}, u32[]{:S(2)}, u32[]{:S(2)}) collective-permute-start(bf16[80,1024]{1,0:T(8,128)(2,1)S(1)} %get-tuple-element.80.refs_0_), channel_id=1, source_target_pairs={{0,8},{8,16},{16,24},{24,32},{32,40},{40,48},{48,56},{56,0},{1,9},... | collective-permute-start | bytes 491528 | tf_op jit(solution)/shard_map/ppermute | solution.py:395
  129.9 5.4 %collective-permute-start.15 = (bf16[80,1024]{1,0:T(8,128)(2,1)S(1)}, bf16[80,1024]{1,0:T(8,128)(2,1)S(1)}, u32[]{:S(2)}, u32[]{:S(2)}) collective-permute-start(bf16[80,1024]{1,0:T(8,128)(2,1)S(1)} %get-tuple-element.84), channel_id=1, source_target_pairs={{0,56},{8,0},{16,8},{24,16},{32,24},{40,32},{48,40},{56,48},{1,57}... | collective-permute-start | bytes 491528 | tf_op jit(solution)/shard_map/ppermute | solution.py:399
  130.0 6.6 %collective-permute-start.16 = (bf16[80,1024]{1,0:T(8,128)(2,1)S(1)}, bf16[80,1024]{1,0:T(8,128)(2,1)S(1)}, u32[]{:S(2)}, u32[]{:S(2)}) collective-permute-start(bf16[80,1024]{1,0:T(8,128)(2,1)S(1)} %get-tuple-element.85), channel_id=1, source_target_pairs={{0,8},{8,16},{16,24},{24,32},{32,40},{40,48},{48,56},{56,0},{1,9},... | collective-permute-start | bytes 491528 | tf_op jit(solution)/shard_map/ppermute | solution.py:395
  136.7 7.5 %collective-permute-start.18 = (bf16[80,1024]{1,0:T(8,128)(2,1)S(1)}, bf16[80,1024]{1,0:T(8,128)(2,1)S(1)}, u32[]{:S(2)}, u32[]{:S(2)}) collective-permute-start(bf16[80,1024]{1,0:T(8,128)(2,1)S(1)} %get-tuple-element.89), channel_id=1, source_target_pairs={{0,8},{8,16},{16,24},{24,32},{32,40},{40,48},{48,56},{56,0},{1,9},... | collective-permute-start | bytes 491528 | tf_op jit(solution)/shard_map/ppermute | solution.py:395
  138.7 6.5 %collective-permute-start.17 = (bf16[80,1024]{1,0:T(8,128)(2,1)S(1)}, bf16[80,1024]{1,0:T(8,128)(2,1)S(1)}, u32[]{:S(2)}, u32[]{:S(2)}) collective-permute-start(bf16[80,1024]{1,0:T(8,128)(2,1)S(1)} %get-tuple-element.88), channel_id=1, source_target_pairs={{0,56},{8,0},{16,8},{24,16},{32,24},{40,32},{48,40},{56,48},{1,57}... | collective-permute-start | bytes 491528 | tf_op jit(solution)/shard_map/ppermute | solution.py:399
  144.2 6.6 %collective-permute-start.19 = (bf16[80,1024]{1,0:T(8,128)(2,1)S(1)}, bf16[80,1024]{1,0:T(8,128)(2,1)S(1)}, u32[]{:S(2)}, u32[]{:S(2)}) collective-permute-start(bf16[80,1024]{1,0:T(8,128)(2,1)S(1)} %hop.5), channel_id=1, source_target_pairs={{0,8},{8,16},{16,24},{24,32},{32,40},{40,48},{48,56},{56,0},{1,9},... | collective-permute-start | bytes 491528 | tf_op jit(solution)/shard_map/ppermute | solution.py:395
